TPU v7x, 256 devices: a whole 4x4x8 slice. The times are simulated.
256 devices in a mesh: section: 2 (over core), dom: 128 (over x, z, y).
Axes of the slice: x: 4, y: 4, z: 8, core: 2. Of those that a mesh axis runs over, the one named last changes fastest.
Arguments:
- node_feats: bfloat16 [2, 32768, 512], P(None, 'dom'), may hold values from -6 to 6
- edge_feats: bfloat16 [2, 65536, 512], P(None, 'dom'), may hold values from -6 to 6
- edge_src: int32 [65536], P('dom'), may hold values from 0 to 511, as said below
- edge_dst: int32 [65536], P('dom'), may hold values from 0 to 255
- edge_count: int32 [128], P('dom'), may hold values from 256 to 512, as said below
- send_rows: int32 [16384, 2], P('dom'), may hold values from 0 to 255
- edge_w1: bfloat16 [2, 3, 512, 512], P('section'), may hold values from -0.15625 to 0.15625
- edge_b1: bfloat16 [2, 512], P('section'), may hold values from -3 to 3
- edge_w2: bfloat16 [2, 512, 512], P('section'), may hold values from -0.25 to 0.25
- edge_gain: bfloat16 [2, 512], P('section'), may hold values from 0.5 to 1.5
- node_w1: bfloat16 [2, 2, 512, 512], P('section'), may hold values from -0.1875 to 0.1875
- node_b1: bfloat16 [2, 512], P('section'), may hold values from -3 to 3
- node_w2: bfloat16 [2, 512, 512], P('section'), may hold values from -0.25 to 0.25
- node_gain: bfloat16 [2, 512], P('section'), may hold values from 0.5 to 1.5
Outputs:
- node_out: bfloat16 [2, 2, 32768, 512], P('section', None, 'dom')
- edge_out: bfloat16 [2, 2, 65536, 512], P('section', None, 'dom')
Inputs may be any that keep to these rules, and one draw needn't show every extreme that they name: `edge_src`: among a device's 512 slots, the first 256 name each value from 256 upward exactly once; the others are below 256. `edge_count`: some device has all 512 slots live.
All inputs are finite; a program needn't handle non-finite values.
Results may differ from a plain program's by a relative error of at most 0.0065.
Values may be sent and summed in bfloat16 or wider, within the bound.
No kernel may reach another device: no remote copies, remote signals or barrier semaphores. Data moves between devices by JAX's collectives and lax.ppermute only.
A program may use at most 64 MiB of HBM per device.

v0:
```python
import jax
import jax.numpy as jnp
from jax import lax
from jax.sharding import PartitionSpec as P


def from_behind(block, axis, distance):
    devices = range(lax.axis_size(axis))
    route = [(i - distance, i) for i in devices if i - distance in devices]
    return lax.ppermute(block, axis, route)


def project(values, weight):
    return jnp.dot(values, weight, preferred_element_type=jnp.float32)


def layer_norm(values, gain):
    row_mean = jnp.mean(values, axis=-1, keepdims=True)
    centred = values - row_mean
    row_var = jnp.mean(centred * centred, axis=-1, keepdims=True)
    return centred * lax.rsqrt(row_var + 1e-05) * gain.astype(jnp.float32)


def apply_layer(node_lat, edge_lat, weights, graph_info):
    edge_w1, edge_b1, edge_w2, edge_gain, node_w1, node_b1, node_w2, node_gain = weights
    edge_src, edge_dst, live_mask, send_rows = graph_info
    outgoing = jnp.take(node_lat, send_rows, axis=0)
    arrived = lax.all_to_all(outgoing, "dom", split_axis=0, concat_axis=0, tiled=True)
    extended = jnp.concatenate([node_lat, arrived.reshape(-1, node_lat.shape[1])], axis=0)
    from_sender = project(extended, edge_w1[1])
    from_receiver = project(node_lat, edge_w1[2])
    hidden = project(edge_lat, edge_w1[0]) + jnp.take(from_sender, edge_src, axis=0)
    hidden = hidden + jnp.take(from_receiver, edge_dst, axis=0) + edge_b1.astype(jnp.float32)
    hidden = jax.nn.silu(hidden).astype(jnp.bfloat16)
    update = layer_norm(project(hidden, edge_w2), edge_gain) * live_mask[:, None]
    message = update.astype(jnp.bfloat16)
    new_edges = (edge_lat.astype(jnp.float32) + update).astype(jnp.bfloat16)
    node_ids = lax.broadcasted_iota(jnp.int32, (node_lat.shape[0], edge_lat.shape[0]), 0)
    onehot = (node_ids == edge_dst[None, :]).astype(jnp.bfloat16)
    incoming = project(onehot, message).astype(jnp.bfloat16)
    node_hidden = (
        project(node_lat, node_w1[0]) + project(incoming, node_w1[1]) + node_b1.astype(jnp.float32)
    )
    node_hidden = jax.nn.silu(node_hidden).astype(jnp.bfloat16)
    node_update = layer_norm(project(node_hidden, node_w2), node_gain)
    new_nodes = (node_lat.astype(jnp.float32) + node_update).astype(jnp.bfloat16)
    return (new_nodes, new_edges)


def local(
    node_feats,
    edge_feats,
    edge_src,
    edge_dst,
    edge_count,
    send_rows,
    edge_w1,
    edge_b1,
    edge_w2,
    edge_gain,
    node_w1,
    node_b1,
    node_w2,
    node_gain,
):
    batches = node_feats.shape[0]
    node_count = node_feats.shape[1]
    edge_slots = edge_feats.shape[1]
    width = node_feats.shape[2]
    section_idx = lax.axis_index("section")
    sections = lax.axis_size("section")
    positions = lax.broadcasted_iota(jnp.int32, (edge_slots,), 0)
    live_mask = (positions < edge_count[0]).astype(jnp.float32)
    graph_info = (edge_src, edge_dst, live_mask, send_rows)
    own_weights = (
        edge_w1[0],
        edge_b1[0],
        edge_w2[0],
        edge_gain[0],
        node_w1[0],
        node_b1[0],
        node_w2[0],
        node_gain[0],
    )
    received = jnp.zeros((node_count + edge_slots, width), jnp.bfloat16)
    results = [received for batch_num in range(batches)]
    ticks = batches + sections - 1
    for tick_num in range(ticks):
        pick = min(tick_num, batches - 1)
        fresh_input = jnp.concatenate([node_feats[pick], edge_feats[pick]], axis=0)
        current = jnp.where(section_idx == 0, fresh_input, received)
        new_nodes, new_edges = apply_layer(
            current[:node_count], current[node_count:], own_weights, graph_info
        )
        combined = jnp.concatenate([new_nodes, new_edges], axis=0)
        for batch_num in range(batches):
            results[batch_num] = jnp.where(
                tick_num - section_idx == batch_num, combined, results[batch_num]
            )
        if tick_num + 1 < ticks:
            received = from_behind(combined, "section", 1)
    stacked = jnp.stack(results)[None]
    return (stacked[:, :, :node_count], stacked[:, :, node_count:])


def solution(mesh):
    in_specs = (
        P(None, "dom", None),
        P(None, "dom", None),
        P("dom"),
        P("dom"),
        P("dom"),
        P("dom", None),
        P("section", None, None, None),
        P("section", None),
        P("section", None, None),
        P("section", None),
        P("section", None, None, None),
        P("section", None),
        P("section", None, None),
        P("section", None),
    )
    out_specs = (P("section", None, "dom", None), P("section", None, "dom", None))
    return jax.shard_map(local, mesh=mesh, in_specs=in_specs, out_specs=out_specs, check_vma=False)
```

profile of v0, /device:TPU:1, one launch (start us, length us, event | category | flops | bytes accessed | tf_op | source)
XLA Modules:
  0.0 135.3 jit_solution(8304900438104815481)
XLA Ops:
  0.7 0.8 compare_select_fusion.2
  1.4 0.7 compare_and_fusion.2
  2.1 2.1 %slice_bitcast_fusion.1 = (bf16[512,512]{1,0:T(8,128)(2,1)}, bf16[512,512]{1,0:T(8,128)(2,1)S(1)}) fusion(bf16[2,512,512]{2,1,0:T(8,128)(2,1)} %param.21), kind=kLoop, calls=%fused_computation.132 | loop fusion | bytes 2097152 | tf_op jit(solution)/shard_map/squeeze | solution.py:90
  4.7 1.2 gather_fusion
  6.1 1.0 broadcast_select_fusion.4
  7.2 16.3 %all-to-all-start = ((bf16[128,2,512]{2,1,0:T(2,128)(2,1)}), bf16[128,2,512]{2,1,0:T(2,128)(2,1)S(1)}, u32[]{:S(2)}, u32[]{:S(2)}) async-start(bf16[128,2,512]{2,1,0:T(2,128)(2,1)} %broadcast_select_fusion.4), calls=%async_computation | async-start | bytes 524288 | tf_op jit(solution)/shard_map/all_to_all | solution.py:28
  23.5 1.3 fusion.52
  25.7 2.3 %gather_fusion.2 = f32[512,512]{1,0:T(8,128)} fusion(f32[256,512]{1,0:T(8,128)S(1)} %fusion.52, s32[1024]{0:T(1024)S(1)} %pad_clamp_fusion), kind=kCustom, calls=%fused_computation.2.clone | custom fusion | bytes 2099200 | tf_op jit(solution)/shard_map/jit(_take)/gather | solution.py:33
  28.0 2.2 %fusion.65 = f32[256,512]{1,0:T(8,128)} fusion(bf16[1,2,512,512]{3,2,1,0:T(8,128)(2,1)} %param.30, bf16[768,512]{1,0:T(8,128)(2,1)S(1)} %maximum_select_fusion), kind=kOutput, calls=%fused_computation.98 | convolution fusion | flops 134217728 | bytes 1310720 | tf_op jit(solution)/shard_map/dot_general | solution.py:14
  30.2 5.8 %all-to-all-done = bf16[128,2,512]{2,1,0:T(2,128)(2,1)S(1)} async-done(((bf16[128,2,512]{2,1,0:T(2,128)(2,1)}), bf16[128,2,512]{2,1,0:T(2,128)(2,1)S(1)}, u32[]{:S(2)}, u32[]{:S(2)}) %all-to-all-start) | async-done | bytes 262176 | tf_op jit(solution)/shard_map/all_to_all | solution.py:28
  36.1 1.5 %fusion.24 = f32[512,512]{1,0:T(8,128)S(1)} fusion(bf16[256,512]{1,0:T(8,128)(2,1)S(1)} %reshape.290, bf16[256,512]{1,0:T(8,128)(2,1)S(1)} %slice.103, bf16[1,3,512,512]{3,2,1,0:T(8,128)(2,1)} %param.26), kind=kOutput, calls=%fused_computation.60 | convolution fusion | flops 269484032 | bytes 2097152 | tf_op jit(solution)/shard_map/dot_general | solution.py:14
  37.6 2.3 %gather_fusion.1 = f32[512,512]{1,0:T(8,128)} fusion(f32[512,512]{1,0:T(8,128)S(1)} %fusion.24, s32[1024]{0:T(1024)S(1)} %pad_clamp_fusion.1), kind=kCustom, calls=%fused_computation.1.clone | custom fusion | bytes 2099200 | tf_op jit(solution)/shard_map/jit(_take)/gather | solution.py:32
  39.9 2.7 %fusion.175 = (f32[512]{0:T(512)S(1)}, f32[512,512]{1,0:T(8,128)S(1)}) fusion(bf16[1,512,512]{2,1,0:T(8,128)(2,1)S(1)} %copy-done, f32[512,512]{1,0:T(8,128)} %gather_fusion.2, f32[512,512]{1,0:T(8,128)} %gather_fusion.1, f32[512]{0:T(512)S(1)} %bitcast.125, pred[512]{0:T(512)(128)(4,1)S(1)} %get-tuple-element.23, ...), kind=kOutput, calls=%fused_computation.210 | convolution fusion | flops 539753984 | bytes 4723712 | tf_op jit(solution)/shard_map/dot_general | solution.py:14
  43.3 2.0 %multiply_convert_fusion.5 = bf16[256,512]{1,0:T(8,128)(2,1)S(1)} fusion(f32[256,512]{1,0:T(8,128)} %fusion.65, f32[512,512]{1,0:T(8,128)S(1)} %get-tuple-element.12, f32[512]{0:T(512)S(1)} %fusion.155, f32[512]{0:T(512)S(1)} %bitcast.117, f32[512]{0:T(512)S(1)} %add_rsqrt_fusion.2, f32[512]{0:T(512)S(1)} %broadcast_multiply_fusion.2, ...), kind=kOutput, calls=%fused_computation.115 | convolution fusion | flops 270925824 | bytes 2371584 | tf_op jit(solution)/shard_map/dot_general | solution.py:14
  45.2 1.4 %fusion.180 = (f32[256]{0:T(256)S(1)}, f32[256,512]{1,0:T(8,128)S(1)}) fusion(bf16[256,512]{1,0:T(8,128)(2,1)S(1)} %multiply_convert_fusion.5, bf16[1,512,512]{2,1,0:T(8,128)(2,1)} %param.32), kind=kOutput, calls=%fused_computation.211 | convolution fusion | flops 134348544 | bytes 1311744 | tf_op jit(solution)/shard_map/dot_general | solution.py:14
  47.2 1.3 collective-permute-start
  48.5 4.8 %collective-permute-done = bf16[768,512]{1,0:T(8,128)(2,1)S(1)} collective-permute-done((bf16[768,512]{1,0:T(8,128)(2,1)S(1)}, bf16[768,512]{1,0:T(8,128)(2,1)S(1)}, u32[]{:S(2)}, u32[]{:S(2)}) %collective-permute-start) | collective-permute-done | bytes 786464 | tf_op jit(solution)/shard_map/ppermute | solution.py:10
  53.5 1.2 gather_fusion.3
  54.8 1.1 broadcast_select_fusion.3
  55.8 6.4 %all-to-all-start.1 = ((bf16[128,2,512]{2,1,0:T(2,128)(2,1)}), bf16[128,2,512]{2,1,0:T(2,128)(2,1)S(1)}, u32[]{:S(2)}, u32[]{:S(2)}) async-start(bf16[128,2,512]{2,1,0:T(2,128)(2,1)} %broadcast_select_fusion.3), calls=%async_computation.1 | async-start | bytes 524288 | tf_op jit(solution)/shard_map/all_to_all | solution.py:28
  62.2 1.3 fusion.50
  63.5 2.3 %gather_fusion.5 = f32[512,512]{1,0:T(8,128)} fusion(f32[256,512]{1,0:T(8,128)S(1)} %fusion.50, s32[1024]{0:T(1024)S(1)} %pad_clamp_fusion), kind=kCustom, calls=%fused_computation.7.clone | custom fusion | bytes 2099200 | tf_op jit(solution)/shard_map/jit(_take)/gather | solution.py:33
  65.8 9.9 %all-to-all-done.1 = bf16[128,2,512]{2,1,0:T(2,128)(2,1)S(1)} async-done(((bf16[128,2,512]{2,1,0:T(2,128)(2,1)}), bf16[128,2,512]{2,1,0:T(2,128)(2,1)S(1)}, u32[]{:S(2)}, u32[]{:S(2)}) %all-to-all-start.1) | async-done | bytes 262176 | tf_op jit(solution)/shard_map/all_to_all | solution.py:28
  75.9 1.5 %fusion.28 = f32[512,512]{1,0:T(8,128)S(1)} fusion(bf16[256,512]{1,0:T(8,128)(2,1)S(1)} %reshape.291, bf16[256,512]{1,0:T(8,128)(2,1)S(1)} %slice.105, bf16[1,3,512,512]{3,2,1,0:T(8,128)(2,1)} %param.26), kind=kOutput, calls=%fused_computation.64 | convolution fusion | flops 269484032 | bytes 2097152 | tf_op jit(solution)/shard_map/dot_general | solution.py:14
  77.4 2.3 %gather_fusion.4 = f32[512,512]{1,0:T(8,128)} fusion(f32[512,512]{1,0:T(8,128)S(1)} %fusion.28, s32[1024]{0:T(1024)S(1)} %pad_clamp_fusion.1), kind=kCustom, calls=%fused_computation.5.clone | custom fusion | bytes 2099200 | tf_op jit(solution)/shard_map/jit(_take)/gather | solution.py:32
  79.7 2.7 %fusion.181 = (f32[512]{0:T(512)S(1)}, f32[512,512]{1,0:T(8,128)S(1)}) fusion(bf16[1,512,512]{2,1,0:T(8,128)(2,1)S(1)} %copy-done, f32[512,512]{1,0:T(8,128)} %gather_fusion.5, f32[512,512]{1,0:T(8,128)} %gather_fusion.4, f32[512]{0:T(512)S(1)} %bitcast.126, pred[512]{0:T(512)(128)(4,1)S(1)} %get-tuple-element.23, ...), kind=kOutput, calls=%fused_computation.212 | convolution fusion | flops 539753984 | bytes 4723712 | tf_op jit(solution)/shard_map/dot_general | solution.py:14
  82.7 2.5 %fusion.9 = f32[256,512]{1,0:T(8,128)} fusion(f32[512,512]{1,0:T(8,128)S(1)} %get-tuple-element.16, f32[512]{0:T(512)S(1)} %add_rsqrt_fusion.1, f32[512]{0:T(512)S(1)} %broadcast_multiply_fusion.1, f32[512]{0:T(512)S(1)} %fusion.155, f32[512]{0:T(512)S(1)} %bitcast.118, bf16[1,2,512,512]{3,2,1,0:T(8,128)(2,1)} %param.30, s32[512]{0:T(512)S(1)} %copy-done.12), kind=kOutput, calls=%fused_computation.28 | convolution fusion | flops 270008320 | bytes 2107392 | tf_op jit(solution)/shard_map/dot_general | solution.py:14
  85.6 2.2 %fusion.186 = (f32[256]{0:T(256)S(1)}, f32[256,512]{1,0:T(8,128)S(1)}) fusion(bf16[1,512,512]{2,1,0:T(8,128)(2,1)} %param.32, f32[256,512]{1,0:T(8,128)} %fusion.9, bf16[1,2,512,512]{3,2,1,0:T(8,128)(2,1)} %param.30, f32[512]{0:T(512)S(1)} %bitcast.123, bf16[768,512]{1,0:T(8,128)(2,1)S(1)} %broadcast_select_fusion.1), kind=kOutput, calls=%fused_computation.213 | convolution fusion | flops 269483776 | bytes 2362368 | tf_op jit(solution)/shard_map/dot_general | solution.py:14
  88.3 1.3 collective-permute-start.1
  89.6 3.4 %collective-permute-done.1 = bf16[768,512]{1,0:T(8,128)(2,1)S(1)} collective-permute-done((bf16[768,512]{1,0:T(8,128)(2,1)S(1)}, bf16[768,512]{1,0:T(8,128)(2,1)S(1)}, u32[]{:S(2)}, u32[]{:S(2)}) %collective-permute-start.1) | collective-permute-done | bytes 786464 | tf_op jit(solution)/shard_map/ppermute | solution.py:10
  93.2 1.2 gather_fusion.6
  94.5 1.0 broadcast_select_fusion.2
  95.6 6.4 %all-to-all-start.2 = ((bf16[128,2,512]{2,1,0:T(2,128)(2,1)}), bf16[128,2,512]{2,1,0:T(2,128)(2,1)S(1)}, u32[]{:S(2)}, u32[]{:S(2)}) async-start(bf16[128,2,512]{2,1,0:T(2,128)(2,1)} %broadcast_select_fusion.2), calls=%async_computation.2 | async-start | bytes 524288 | tf_op jit(solution)/shard_map/all_to_all | solution.py:28
  102.0 1.3 fusion.48
  103.3 2.3 %gather_fusion.8 = f32[512,512]{1,0:T(8,128)} fusion(f32[256,512]{1,0:T(8,128)S(1)} %fusion.48, s32[1024]{0:T(1024)S(1)} %pad_clamp_fusion), kind=kCustom, calls=%fused_computation.8.clone | custom fusion | bytes 2099200 | tf_op jit(solution)/shard_map/jit(_take)/gather | solution.py:33
  105.6 9.8 %all-to-all-done.2 = bf16[128,2,512]{2,1,0:T(2,128)(2,1)S(1)} async-done(((bf16[128,2,512]{2,1,0:T(2,128)(2,1)}), bf16[128,2,512]{2,1,0:T(2,128)(2,1)S(1)}, u32[]{:S(2)}, u32[]{:S(2)}) %all-to-all-start.2) | async-done | bytes 262176 | tf_op jit(solution)/shard_map/all_to_all | solution.py:28
  115.5 0.8 reshape.292
  116.3 1.6 %fusion.32 = f32[512,512]{1,0:T(8,128)S(1)} fusion(bf16[256,512]{1,0:T(8,128)(2,1)} %reshape.292, bf16[256,512]{1,0:T(8,128)(2,1)S(1)} %slice.107, bf16[1,3,512,512]{3,2,1,0:T(8,128)(2,1)} %param.26), kind=kOutput, calls=%fused_computation.68 | convolution fusion | flops 269484032 | bytes 2097152 | tf_op jit(solution)/shard_map/dot_general | solution.py:14
  117.8 2.3 %gather_fusion.7 = f32[512,512]{1,0:T(8,128)} fusion(f32[512,512]{1,0:T(8,128)S(1)} %fusion.32, s32[1024]{0:T(1024)S(1)} %pad_clamp_fusion.1), kind=kCustom, calls=%fused_computation.6.clone | custom fusion | bytes 2099200 | tf_op jit(solution)/shard_map/jit(_take)/gather | solution.py:32
  120.2 3.8 %fusion.191 = (f32[512]{0:T(512)S(1)}, f32[512,512]{0,1:T(8,128)}) fusion(bf16[1,512,512]{2,1,0:T(8,128)(2,1)S(1)} %copy-done, f32[512,512]{1,0:T(8,128)} %gather_fusion.8, f32[512,512]{1,0:T(8,128)} %gather_fusion.7, f32[512]{0:T(512)S(1)} %bitcast.127, pred[512]{0:T(512)(128)(4,1)S(1)} %get-tuple-element.23, pred[512]{0:T(512)(128)(4,1)S(1)} %get-tuple-element.24, ...), kind=kOutput, calls=%fused_computation.214 | convolution fusion | flops 539753984 | bytes 4723712 | tf_op jit(solution)/shard_map/dot_general | solution.py:14
  124.0 1.6 %copy.26 = f32[512,512]{1,0:T(8,128)S(1)} copy(f32[512,512]{0,1:T(8,128)} %get-tuple-element.20) | data formatting | bytes 2097152 | tf_op jit(solution)/shard_map/dot_general | solution.py:14
  125.8 2.5 %fusion.10 = f32[256,512]{1,0:T(8,128)} fusion(f32[512,512]{1,0:T(8,128)S(1)} %copy.26, f32[512]{0:T(512)S(1)} %add_rsqrt_fusion, f32[512]{0:T(512)S(1)} %broadcast_multiply_fusion, f32[512]{0:T(512)S(1)} %fusion.155, f32[512]{0:T(512)S(1)} %bitcast.120, bf16[1,2,512,512]{3,2,1,0:T(8,128)(2,1)} %param.30, s32[512]{0:T(512)S(1)} %copy-done.12), kind=kOutput, calls=%fused_computation.29 | convolution fusion | flops 270008320 | bytes 2107392 | tf_op jit(solution)/shard_map/dot_general | solution.py:14
  128.4 1.1 fusion.23
  129.5 2.0 %fusion.196 = (f32[256]{0:T(256)S(1)}, f32[256,512]{1,0:T(8,128)S(1)}) fusion(bf16[1,512,512]{2,1,0:T(8,128)(2,1)} %param.32, f32[256,512]{1,0:T(8,128)} %fusion.10, bf16[1,2,512,512]{3,2,1,0:T(8,128)(2,1)} %param.30, f32[512]{0:T(512)S(1)} %bitcast.124, bf16[768,512]{1,0:T(8,128)(2,1)S(1)} %broadcast_select_fusion), kind=kOutput, calls=%fused_computation.215 | convolution fusion | flops 269483776 | bytes 2362368 | tf_op jit(solution)/shard_map/dot_general | solution.py:14
  131.9 0.6 copy-done.4
  132.8 0.5 select_select_fusion.1
  133.5 1.0 slice.110
  134.5 0.8 slice.109
  (85 shorter events, 4.9 us)
Async XLA Ops:
  0.6 39.3 %copy-start = (bf16[1,512,512]{2,1,0:T(8,128)(2,1)S(1)}, bf16[1,512,512]{2,1,0:T(8,128)(2,1)}, u32[]{:S(2)}) copy-start(bf16[1,512,512]{2,1,0:T(8,128)(2,1)} %param.28) | copy-start | bytes 1572868
  0.6 3.5 %copy-start.10 = (bf16[2,256,512]{2,1,0:T(8,128)(2,1)S(1)}, bf16[2,256,512]{2,1,0:T(8,128)(2,1)}, u32[]{:S(2)}) copy-start(bf16[2,256,512]{2,1,0:T(8,128)(2,1)} %param.20) | copy-start | bytes 1572868
  4.2 49.0 %copy-start.5 = (bf16[256,512]{1,0:T(8,128)(2,1)}, bf16[256,512]{1,0:T(8,128)(2,1)S(1)}, u32[]{:S(2)}) copy-start(bf16[256,512]{1,0:T(8,128)(2,1)S(1)} %get-tuple-element.9) | copy-start | bytes 786436
  4.7 18.8 %copy-start.11 = (s32[512]{0:T(512)S(1)}, s32[512]{0:T(512)}, u32[]{:S(2)}) copy-start(s32[512]{0:T(512)} %param.22) | copy-start | bytes 6148
  5.8 19.1 %copy-start.12 = (s32[512]{0:T(512)S(1)}, s32[512]{0:T(512)}, u32[]{:S(2)}) copy-start(s32[512]{0:T(512)} %param.23) | copy-start | bytes 6148
  5.8 19.7 %copy-start.13 = (bf16[1,512]{1,0:T(2,128)(2,1)S(1)}, bf16[1,512]{1,0:T(2,128)(2,1)}, u32[]{:S(2)}) copy-start(bf16[1,512]{1,0:T(2,128)(2,1)} %param.27) | copy-start | bytes 3076
  5.9 19.7 %copy-start.14 = (bf16[1,512]{1,0:T(2,128)(2,1)S(1)}, bf16[1,512]{1,0:T(2,128)(2,1)}, u32[]{:S(2)}) copy-start(bf16[1,512]{1,0:T(2,128)(2,1)} %param.29) | copy-start | bytes 3076
  5.9 19.8 %copy-start.15 = (bf16[1,512]{1,0:T(2,128)(2,1)S(1)}, bf16[1,512]{1,0:T(2,128)(2,1)}, u32[]{:S(2)}) copy-start(bf16[1,512]{1,0:T(2,128)(2,1)} %param.31) | copy-start | bytes 3076
  5.9 19.8 %copy-start.16 = (bf16[1,512]{1,0:T(2,128)(2,1)S(1)}, bf16[1,512]{1,0:T(2,128)(2,1)}, u32[]{:S(2)}) copy-start(bf16[1,512]{1,0:T(2,128)(2,1)} %param.33) | copy-start | bytes 3076
  7.2 28.8 %all-to-all-start = ((bf16[128,2,512]{2,1,0:T(2,128)(2,1)}), bf16[128,2,512]{2,1,0:T(2,128)(2,1)S(1)}, u32[]{:S(2)}, u32[]{:S(2)}) async-start(bf16[128,2,512]{2,1,0:T(2,128)(2,1)} %broadcast_select_fusion.4), calls=%async_computation | async-start | bytes 524288 | tf_op jit(solution)/shard_map/all_to_all | solution.py:28
  46.7 6.6 %copy-start.1 = (bf16[512,512]{1,0:T(8,128)(2,1)S(1)}, bf16[512,512]{1,0:T(8,128)(2,1)}, u32[]{:S(2)}) copy-start(bf16[512,512]{1,0:T(8,128)(2,1)} %get-tuple-element.7) | copy-start | bytes 1572868
  47.1 6.2 %copy-start.7 = (bf16[256,512]{1,0:T(8,128)(2,1)}, bf16[256,512]{1,0:T(8,128)(2,1)S(1)}, u32[]{:S(2)}) copy-start(bf16[256,512]{1,0:T(8,128)(2,1)S(1)} %add_convert_fusion.5) | copy-start | bytes 786436
  47.2 6.1 %collective-permute-start = (bf16[768,512]{1,0:T(8,128)(2,1)S(1)}, bf16[768,512]{1,0:T(8,128)(2,1)S(1)}, u32[]{:S(2)}, u32[]{:S(2)}) collective-permute-start(bf16[768,512]{1,0:T(8,128)(2,1)S(1)} %pad_maximum_fusion.1), channel_id=1, source_target_pairs={{0,128},{1,129},{2,130},{3,131},{4,132},{5,133},{6,134},{7,135},{8... | collective-permute-start | bytes 2359304 | tf_op jit(solution)/shard_map/ppermute | solution.py:10
  55.8 20.0 %all-to-all-start.1 = ((bf16[128,2,512]{2,1,0:T(2,128)(2,1)}), bf16[128,2,512]{2,1,0:T(2,128)(2,1)S(1)}, u32[]{:S(2)}, u32[]{:S(2)}) async-start(bf16[128,2,512]{2,1,0:T(2,128)(2,1)} %broadcast_select_fusion.3), calls=%async_computation.1 | async-start | bytes 524288 | tf_op jit(solution)/shard_map/all_to_all | solution.py:28
  85.6 2.7 %copy-start.3 = (bf16[512,512]{1,0:T(8,128)(2,1)}, bf16[512,512]{1,0:T(8,128)(2,1)S(1)}, u32[]{:S(2)}) copy-start(bf16[512,512]{1,0:T(8,128)(2,1)S(1)} %add_convert_fusion.1) | copy-start | bytes 1572868
  87.8 5.2 %copy-start.2 = (bf16[512,512]{1,0:T(8,128)(2,1)S(1)}, bf16[512,512]{1,0:T(8,128)(2,1)}, u32[]{:S(2)}) copy-start(bf16[512,512]{1,0:T(8,128)(2,1)} %get-tuple-element.7) | copy-start | bytes 1572868
  87.8 5.2 %copy-start.6 = (bf16[256,512]{1,0:T(8,128)(2,1)S(1)}, bf16[256,512]{1,0:T(8,128)(2,1)}, u32[]{:S(2)}) copy-start(bf16[256,512]{1,0:T(8,128)(2,1)} %copy-done.5) | copy-start | bytes 786436
  88.3 4.7 %collective-permute-start.1 = (bf16[768,512]{1,0:T(8,128)(2,1)S(1)}, bf16[768,512]{1,0:T(8,128)(2,1)S(1)}, u32[]{:S(2)}, u32[]{:S(2)}) collective-permute-start(bf16[768,512]{1,0:T(8,128)(2,1)S(1)} %pad_maximum_fusion.2), channel_id=1, source_target_pairs={{0,128},{1,129},{2,130},{3,131},{4,132},{5,133},{6,134},{7,135},{8... | collective-permute-start | bytes 2359304 | tf_op jit(solution)/shard_map/ppermute | solution.py:10
  95.6 19.9 %all-to-all-start.2 = ((bf16[128,2,512]{2,1,0:T(2,128)(2,1)}), bf16[128,2,512]{2,1,0:T(2,128)(2,1)S(1)}, u32[]{:S(2)}, u32[]{:S(2)}) async-start(bf16[128,2,512]{2,1,0:T(2,128)(2,1)} %broadcast_select_fusion.2), calls=%async_computation.2 | async-start | bytes 524288 | tf_op jit(solution)/shard_map/all_to_all | solution.py:28
  131.5 1.0 copy-start.4
  131.5 1.1 copy-start.8
  131.5 1.3 copy-start.9
where the time goes:
time: 136 us; the launch traced here: 135 us
  waiting for transfers between devices  33.8 us (25%)
  matrix products  32.6 us (24%)
  starting transfers between devices  31.7 us (23%)
  local copies, waits for them, and re-layouts  25.7 us (19%)
  other arithmetic  9.75 us (7%)
  between operations  1.89 us (1%)
    dot_general x16, matrix products, project(): return jnp.dot(values, weight, preferred_element_type=jnp.float32)  32.6 us
    all_to_all x3, starting transfers between devices, apply_layer(): lax.all_to_all(outgoing, 'dom', split_axis=0, concat_axis=0, tiled=True)  29.1 us
    all_to_all x3, waiting for transfers between devices, apply_layer(): lax.all_to_all(outgoing, 'dom', split_axis=0, concat_axis=0, tiled=True)  25.6 us
    ppermute x2, waiting for transfers between devices, from_behind(): return lax.ppermute(block, axis, route)  8.19 us
    gather x3, local copies, waits for them, and re-layouts, apply_layer(): jnp.take(from_sender, edge_src, axis=0)  7.03 us
    gather x3, local copies, waits for them, and re-layouts, apply_layer(): jnp.take(from_receiver, edge_dst, axis=0)  6.98 us
    select_n x4, other arithmetic, apply_layer(): outgoing = jnp.take(node_lat, send_rows, axis=0)  3.9 us
    gather x6, local copies, waits for them, and re-layouts, apply_layer(): outgoing = jnp.take(node_lat, send_rows, axis=0)  3.77 us
  transfers between devices with their start and end apart: 5, of which 5 were waited for; matrix products, arithmetic and copies ran while one was open for 10% of the time, Pallas kernels for 0%

commit v1 on v0

v1 whole, which is shorter than its diff:
```python
import functools

import jax
import jax.numpy as jnp
from jax import lax
from jax.experimental import pallas as pl
from jax.experimental.pallas import tpu as pltpu
from jax.sharding import PartitionSpec as P


F32 = jnp.float32
BF16 = jnp.bfloat16
VMEM = pl.BlockSpec(memory_space=pltpu.VMEM)
SMEM = pl.BlockSpec(memory_space=pltpu.SMEM)
ANY = pl.BlockSpec(memory_space=pl.ANY)
LIMIT = 67043328


def dot(a, b):
    return jnp.dot(a, b, preferred_element_type=F32)


def dot_ta(a, b):
    return lax.dot_general(a, b, (((0,), (0,)), ((), ())), preferred_element_type=F32)


def dot_tb(a, b):
    return lax.dot_general(a, b, (((1,), (1,)), ((), ())), preferred_element_type=F32)


def silu(x):
    half = 0.5 * x
    return half + half * jnp.tanh(half)


def centre(y):
    c = y - jnp.mean(y, axis=-1, keepdims=True)
    var = jnp.mean(c * c, axis=-1, keepdims=True)
    return c * lax.rsqrt(var + 1e-05)


def pick_onehot(row, ids):
    return (ids == row).astype(F32).astype(BF16)


def sublane_ids(rows, cols):
    return lax.broadcasted_iota(jnp.int32, (rows, cols), 0)


def arrival_ids(half, peers, first):
    q = sublane_ids(half, half)
    return first + (half // peers) * (q % peers) + q // peers


def send_onehot(idx, nodes):
    row = jnp.concatenate([idx[k : k + 1] for k in range(idx.shape[0])], axis=1)
    return pick_onehot(row, sublane_ids(nodes, row.shape[1]))


def pack_rows(picked, msg, tmp, peers):
    per, lanes = picked.shape[0] // peers, picked.shape[1] // 128
    for k in range(per):
        for c in range(lanes):
            tmp[pl.ds(k * lanes + c, peers, stride=per * lanes), :] = (
                picked[k * peers : (k + 1) * peers, c * 128 : (c + 1) * 128])
    msg[...] = tmp[...].astype(BF16)


def unpack_rows(msg, tmp, half, width, peers):
    per, lanes = half // peers, width // 128
    tmp[...] = msg[...].astype(F32)
    blocks = [
        jnp.concatenate(
            [tmp[pl.ds(k * lanes + c, peers, stride=per * lanes), :] for c in range(lanes)], axis=1)
        for k in range(per)
    ]
    return jnp.concatenate(blocks, axis=0).astype(BF16)


def start(pairs, sems):
    copies = [pltpu.make_async_copy(a, b, sems.at[i]) for i, (a, b) in enumerate(pairs)]
    for c in copies:
        c.start()
    return copies


def wait(copies):
    for c in copies:
        c.wait()


def matrices(refs):
    ew1, ew2, nw1, nw2 = refs
    return ew1.at[0, 0], ew1.at[0, 1], ew1.at[0, 2], ew2.at[0], nw1.at[0, 0], nw1.at[0, 1], nw2.at[0]


def fetch_weights(mine, own, oth, which, w, sems):
    @pl.when(mine)
    def _():
        start([(matrices(own)[k], w.at[i]) for i, k in enumerate(which)], sems)

    @pl.when(jnp.logical_not(mine))
    def _():
        start([(matrices(oth)[k], w.at[i]) for i, k in enumerate(which)], sems)

    return [pltpu.make_async_copy(matrices(own)[k], w.at[i], sems.at[i]) for i, k in enumerate(which)]


LOCAL = (0, 1, 2, 3, 4)
FINISH = (1, 3, 5, 6)


def select_kernel(peers, sec, idx_h, feats, msg_h, idx, lat, msg, tmp, sems):
    c_idx, c_lat = start(((idx_h, idx), (feats.at[sec[0]], lat)), sems)
    c_idx.wait()
    oh = send_onehot(idx[...], lat.shape[0])
    c_lat.wait()
    pack_rows(dot_ta(oh, lat[...]), msg, tmp, peers)
    wait(start(((msg, msg_h),), sems))


def local_work(count, src, dst, v, e_halo, e_local, w, vec, oh_q, outs):
    pre_q, part, pre_n = outs
    half = src.shape[1] // 2
    nodes = v.shape[0]
    ids = sublane_ids(nodes, half)
    recv_l = pick_onehot(dst[:, half:], ids)
    send_l = pick_onehot(src[:, half:], ids)
    vs_l = dot_ta(send_l, v).astype(BF16)
    vr_l = dot_ta(recv_l, v).astype(BF16)
    vr_q = dot_ta(oh_q, v).astype(BF16)
    pre_q[...] = dot(e_halo, w[0]) + dot(vr_q, w[2]) + vec[0:1]
    h = dot(e_local, w[0]) + dot(vs_l, w[1]) + dot(vr_l, w[2]) + vec[0:1]
    y = centre(dot(silu(h).astype(BF16), w[3])) * vec[1:2]
    pos = sublane_ids(half, 1) + half
    upd = jnp.where(pos < count[0], y, 0.0)
    part[...] = dot(recv_l, upd.astype(BF16))
    pre_n[...] = dot(v, w[4]) + vec[2:3]
    return (e_local.astype(F32) + upd).astype(BF16)


def pick_vec(mine, vec_own, vec_oth):
    return jnp.where(mine, vec_own[...].astype(F32), vec_oth[...].astype(F32))


def first_local_kernel(peers, sec, count, src_h, dst_h, idx_h, nfeats, efeats, ew1, ew2, nw1, nw2,
                       xew1, xew2, xnw1, xnw2, vo_h, vx_h,
                       pre_q_h, part_h, pre_n_h, e1_loc_h, lat_h, e_q_h, oh_q_h, oh_s_h, perm_h, live_h,
                       src, dst, idx, vo, vx, lat, e, w, pre_q, part, pre_n, e1_loc, e_q, oh_q, oh_s, perm_q, live_q,
                       sem_w, sem_in, sem_out):
    half = src.shape[1] // 2
    nodes = lat.shape[0]
    mine = sec[0] == 0
    ins = start(((src_h, src), (dst_h, dst), (idx_h, idx), (efeats.at[sec[0]], e), (nfeats.at[sec[0]], lat),
                 (vo_h, vo), (vx_h, vx)), sem_in)
    weights = fetch_weights(mine, (ew1, ew2, nw1, nw2), (xew1, xew2, xnw1, xnw2), LOCAL, w, sem_w)
    wait(ins)
    oh_s[...] = send_onehot(idx[...], nodes)
    perm = pick_onehot(src[:, :half], arrival_ids(half, peers, nodes))
    perm_q[...] = perm
    recv_h = pick_onehot(dst[:, :half], sublane_ids(nodes, half))
    ohq = dot_tb(recv_h, perm).astype(BF16)
    oh_q[...] = ohq
    pos = lax.broadcasted_iota(jnp.int32, (half, half), 1)
    live = jnp.sum(jnp.where(pos < count[0], perm.astype(F32), 0.0), axis=1, keepdims=True)
    live_q[...] = jnp.broadcast_to(live, live_q.shape)
    eq = dot(perm, e[:half]).astype(BF16)
    e_q[...] = eq
    wait(weights)
    e1_loc[...] = local_work(count, src, dst, lat[...], eq, e[half:], w, pick_vec(mine, vo, vx), ohq,
                             (pre_q, part, pre_n))
    wait(start(((pre_q, pre_q_h), (part, part_h), (pre_n, pre_n_h), (e1_loc, e1_loc_h), (lat, lat_h), (e_q, e_q_h),
                (oh_q, oh_q_h), (oh_s, oh_s_h), (perm_q, perm_h), (live_q, live_h)), sem_out))


def second_local_kernel(sec, count, src_h, dst_h, lat_h, e_q_h, e_loc_h, oh_q_h, perm_h, ew1, ew2, nw1, nw2,
                        xew1, xew2, xnw1, xnw2, vo_h, vx_h,
                        pre_q_h, part_h, pre_n_h, e1_h_h, out_l_h, n_out, e_out,
                        src, dst, vo, vx, lat, e_q, e_loc, oh_q, perm_q, w, pre_q, part, pre_n, e1_h, own_l, out_l,
                        sem_w, sem_in, sem_out):
    half = src.shape[1] // 2
    mine = sec[0] == 1
    ins = start(((src_h, src), (dst_h, dst), (lat_h, lat), (e_q_h, e_q), (e_loc_h, e_loc), (oh_q_h, oh_q),
                 (perm_h, perm_q), (vo_h, vo), (vx_h, vx)), sem_in)
    weights = fetch_weights(mine, (ew1, ew2, nw1, nw2), (xew1, xew2, xnw1, xnw2), LOCAL, w, sem_w)
    wait(ins)
    eq = e_q[...]
    e1_h[...] = dot_ta(perm_q[...], eq).astype(BF16)
    wait(weights)
    first = e_loc[...]
    second = local_work(count, src, dst, lat[...], eq, first, w, pick_vec(mine, vo, vx), oh_q[...],
                        (pre_q, part, pre_n))

    @pl.when(mine)
    def _():
        own_l[...] = second
        out_l[...] = first

    @pl.when(jnp.logical_not(mine))
    def _():
        own_l[...] = first
        out_l[...] = second

    wait(start(((pre_q, pre_q_h), (part, part_h), (pre_n, pre_n_h), (e1_h, e1_h_h), (out_l, out_l_h),
                (own_l, e_out.at[0, sec[0], pl.ds(half, half)])), sem_out))


def finish(peers, mine, refs, tmp, weights, ins):
    msg, pre_q, vo, vx, live_q, oh_q, part, pre_n, e_q, lat, w = refs
    c_msg, c_pre, c_vo, c_vx, c_live, c_ohq, c_part, c_pren, c_eq, c_lat = ins
    c_msg.wait()
    halo = unpack_rows(msg, tmp, e_q.shape[0], e_q.shape[1], peers)
    wait((c_pre, c_vo, c_vx, weights[0]))
    vec = pick_vec(mine, vo, vx)
    h = pre_q[...] + dot(halo, w[0])
    hid = silu(h).astype(BF16)
    wait((weights[1], c_live, c_ohq, c_part, c_eq))
    y = centre(dot(hid, w[1])) * vec[1:2]
    upd = jnp.where(live_q[:, 0:1] > 0.5, y, 0.0)
    incoming = (part[...] + dot(oh_q[...], upd.astype(BF16))).astype(BF16)
    new_e = (e_q[...].astype(F32) + upd).astype(BF16)
    wait((weights[2], weights[3], c_pren, c_lat))
    hn = silu(pre_n[...] + dot(incoming, w[2])).astype(BF16)
    yn = centre(dot(hn, w[3])) * vec[3:4]
    new_n = (lat[...].astype(F32) + yn).astype(BF16)
    return new_n, new_e


def start_finish(mine, hbm, vmem, own, oth, w, sem_in, sem_w):
    first = start(((hbm[0], vmem[0]),), sem_in)
    weights = fetch_weights(mine, own, oth, FINISH, w, sem_w)
    rest = [pltpu.make_async_copy(a, b, sem_in.at[i + 1]) for i, (a, b) in enumerate(zip(hbm[1:], vmem[1:]))]
    for c in rest:
        c.start()
    return first + rest, weights


def first_finish_kernel(peers, sec, msg_h, pre_q_h, vo_h, vx_h, live_h, oh_q_h, part_h, pre_n_h, e_q_h, lat_h, oh_s_h,
                        ew1, ew2, nw1, nw2, xew1, xew2, xnw1, xnw2, out_msg_h, new_n_h, new_e_h,
                        msg, pre_q, vo, vx, live_q, oh_q, part, pre_n, e_q, lat, oh_s, w, tmp, out_msg, new_n, new_e,
                        sem_w, sem_in, sem_out):
    mine = sec[0] == 0
    hbm = (msg_h, pre_q_h, vo_h, vx_h, live_h, oh_q_h, part_h, pre_n_h, e_q_h, lat_h, oh_s_h)
    vmem = (msg, pre_q, vo, vx, live_q, oh_q, part, pre_n, e_q, lat, oh_s)
    ins, weights = start_finish(mine, hbm, vmem, (ew1, ew2, nw1, nw2), (xew1, xew2, xnw1, xnw2), w, sem_in, sem_w)
    n, e = finish(peers, mine, vmem[:10] + (w,), tmp, weights, ins[:10])
    new_n[...] = n
    new_e[...] = e
    ins[10].wait()
    pack_rows(dot_ta(oh_s[...], n), out_msg, tmp, peers)
    wait(start(((out_msg, out_msg_h), (new_n, new_n_h), (new_e, new_e_h)), sem_out))


def last_finish_kernel(peers, sec, msg_h, pre_q_h, vo_h, vx_h, live_h, oh_q_h, part_h, pre_n_h, e_q_h, lat_h,
                       perm_h, e1_h_h, ew1, ew2, nw1, nw2, xew1, xew2, xnw1, xnw2, n_in, e_in,
                       out_n_h, out_h_h, n_out, e_out,
                       msg, pre_q, vo, vx, live_q, oh_q, part, pre_n, e_q, lat, perm_q, e1_h, w, tmp, new_n, new_h,
                       sem_w, sem_in, sem_out):
    mine = sec[0] == 1
    half = e_q.shape[0]
    hbm = (msg_h, pre_q_h, vo_h, vx_h, live_h, oh_q_h, part_h, pre_n_h, e_q_h, lat_h, perm_h, e1_h_h)
    vmem = (msg, pre_q, vo, vx, live_q, oh_q, part, pre_n, e_q, lat, perm_q, e1_h)
    ins, weights = start_finish(mine, hbm, vmem, (ew1, ew2, nw1, nw2), (xew1, xew2, xnw1, xnw2), w, sem_in, sem_w)
    n, e = finish(peers, mine, vmem[:10] + (w,), tmp, weights, ins[:10])
    new_n[...] = n
    wait(ins[10:])
    new_h[...] = dot_ta(perm_q[...], e).astype(BF16)
    own_n = n_out.at[0, sec[0]]
    own_h = e_out.at[0, sec[0], pl.ds(0, half)]

    @pl.when(mine)
    def _():
        start(((new_n, own_n), (new_h, own_h), (lat, out_n_h), (e1_h, out_h_h)), sem_out)

    @pl.when(jnp.logical_not(mine))
    def _():
        start(((new_n, out_n_h), (new_h, out_h_h), (lat, own_n), (e1_h, own_h)), sem_out)

    wait([pltpu.make_async_copy(a, b, sem_out.at[i]) for i, (a, b) in enumerate(
        ((new_n, out_n_h), (new_h, out_h_h), (lat, own_n), (e1_h, own_h)))])


def other_out_kernel(sec, oth_n, oth_h, oth_l, n_in, e_in, n_out, e_out, sems):
    half = oth_h.shape[0]
    other = 1 - sec[0]
    wait(start((
        (oth_n, n_out.at[0, other]),
        (oth_h, e_out.at[0, other, pl.ds(0, half)]),
        (oth_l, e_out.at[0, other, pl.ds(half, half)]),
    ), sems))


def call(kernel, in_specs, out_specs, out_shapes, scratch, flops, nbytes, limit=LIMIT, **kw):
    return pl.pallas_call(
        kernel,
        out_shape=out_shapes,
        in_specs=in_specs,
        out_specs=out_specs,
        scratch_shapes=scratch,
        compiler_params=pltpu.CompilerParams(vmem_limit_bytes=limit),
        cost_estimate=pl.CostEstimate(flops=flops, bytes_accessed=nbytes, transcendentals=0),
        **kw,
    )


def vmem(x):
    return pltpu.VMEM(x.shape, x.dtype)


def layers(node_feats, edge_feats, edge_src, edge_dst, edge_count, send_rows,
           edge_w1, edge_b1, edge_w2, edge_gain, node_w1, node_b1, node_w2, node_gain):
    _, nodes, width = node_feats.shape
    slots = edge_feats.shape[1]
    half = slots // 2
    peers = send_rows.shape[0]
    sec = lax.axis_index("section").astype(jnp.int32).reshape(1)
    idx = send_rows.T
    src = edge_src.reshape(1, -1)
    dst = edge_dst.reshape(1, -1)
    shape = jax.ShapeDtypeStruct
    nb, nf = shape((nodes, width), BF16), shape((nodes, width), F32)
    hb, hf = shape((half, width), BF16), shape((half, width), F32)
    onehot = shape((nodes, half), BF16)
    live = shape((half, 128), F32)
    msg = shape((half * width // 128, 128), BF16)
    tmp = pltpu.VMEM(msg.shape, F32)
    wts = lambda n: pltpu.VMEM((n, width, width), BF16)
    outs = [shape((1, 2, nodes, width), BF16), shape((1, 2, slots, width), BF16)]

    def DMA(n):
        return pltpu.SemaphoreType.DMA((n,))

    def halo_exchange(m):
        got = lax.all_to_all(m.reshape(peers, -1, 128), "dom", split_axis=0, concat_axis=0, tiled=True)
        return got.reshape(-1, 128)

    def swap(x):
        return lax.ppermute(x, "section", [(0, 1), (1, 0)])

    rows = call(
        functools.partial(select_kernel, peers), [SMEM, ANY, ANY], ANY, msg,
        [vmem(idx), vmem(nb), vmem(msg), tmp, DMA(2)], 10**8, 10**6,
    )(sec, idx, node_feats)
    halo = halo_exchange(rows)
    own_w = (edge_w1, edge_w2, node_w1, node_w2)
    oth_w = []
    for x in own_w:
        oth_w.append(swap(x))
    vec = jnp.concatenate([edge_b1, edge_gain, node_b1, node_gain], axis=0)
    oth_vec = swap(vec)

    res = [hf, nf, nf, hb, nb, hb, onehot, onehot, onehot, live]
    pre_q, part, pre_n, e1_loc, lat, e_q, oh_q, oh_s, perm_q, live_q = call(
        functools.partial(first_local_kernel, peers), [SMEM, SMEM] + [ANY] * 15, [ANY] * 10, res,
        [vmem(x) for x in (src, dst, idx, vec, vec, nb)] + [pltpu.VMEM((slots, width), BF16), wts(5)]
        + [vmem(x) for x in (hf, nf, nf, hb, hb, onehot, onehot, onehot, live)] + [DMA(5), DMA(7), DMA(10)],
        2 * 10**9, 10**7,
    )(sec, edge_count, src, dst, idx, node_feats, edge_feats, *own_w, *oth_w, vec, oth_vec)

    args = (halo, pre_q, vec, oth_vec, live_q, oh_q, part, pre_n, e_q, lat, oh_s)
    rows, n1, e1_q = call(
        functools.partial(first_finish_kernel, peers), [SMEM] + [ANY] * 19, [ANY] * 3, [msg, nb, hb],
        [vmem(x) for x in args] + [wts(4), tmp, vmem(msg), vmem(nb), vmem(hb), DMA(4), DMA(11), DMA(3)],
        10**9, 4 * 10**6,
    )(sec, *args, *own_w, *oth_w)
    halo = halo_exchange(rows)

    args = (n1, e1_q, e1_loc, oh_q, perm_q)
    pre_q, part, pre_n, e1_h, out_l, n_out, e_out = call(
        second_local_kernel, [SMEM, SMEM] + [ANY] * 17, [ANY] * 7, [hf, nf, nf, hb, hb] + outs,
        [vmem(x) for x in (src, dst, vec, vec) + args] + [wts(5)] + [vmem(x) for x in (hf, nf, nf, hb, hb, hb)]
        + [DMA(5), DMA(9), DMA(6)],
        2 * 10**9, 10**7,
    )(sec, edge_count, src, dst, *args, *own_w, *oth_w, vec, oth_vec)
    oth_l = swap(out_l)

    args = (halo, pre_q, vec, oth_vec, live_q, oh_q, part, pre_n, e1_q, n1, perm_q, e1_h)
    out_n, out_h, n_out, e_out = call(
        functools.partial(last_finish_kernel, peers), [SMEM] + [ANY] * 22, [ANY] * 4, [nb, hb] + outs,
        [vmem(x) for x in args] + [wts(4), tmp, vmem(nb), vmem(hb), DMA(4), DMA(12), DMA(4)],
        10**9, 4 * 10**6, input_output_aliases={21: 2, 22: 3},
    )(sec, *args, *own_w, *oth_w, n_out, e_out)
    oth_h = swap(out_h)
    oth_n = swap(out_n)

    return call(other_out_kernel, [SMEM] + [VMEM] * 3 + [ANY, ANY], [ANY, ANY], outs, [DMA(3)], 0, 3 * 10**6,
                limit=1024 * 1024, input_output_aliases={4: 0, 5: 1})(sec, oth_n, oth_h, oth_l, n_out, e_out)


def solution(mesh):
    in_specs = (
        P(None, "dom", None),
        P(None, "dom", None),
        P("dom"),
        P("dom"),
        P("dom"),
        P("dom", None),
        P("section", None, None, None),
        P("section", None),
        P("section", None, None),
        P("section", None),
        P("section", None, None, None),
        P("section", None),
        P("section", None, None),
        P("section", None),
    )
    out_specs = (P("section", None, "dom", None), P("section", None, "dom", None))
    return jax.shard_map(layers, mesh=mesh, in_specs=in_specs, out_specs=out_specs, check_vma=False)
```

time: 136 us -> 72.9 us (0.54)
  matrix products: 32.6 us -> 0 us
  Pallas kernels: 0 us -> 25 us
  local copies, waits for them, and re-layouts: 25.7 us -> 1.17 us
  waiting for transfers between devices: 33.8 us -> 10.2 us
  other arithmetic: 9.75 us -> 0.75 us
  starting transfers between devices: 31.7 us -> 33.9 us
    dot_general x16 -> x0, matrix products: 32.6 us -> none  [project(): return jnp.dot(values, weight, preferred_element_type=jnp.float32)]
    pallas_call x0 -> x6, Pallas kernels: none -> 25 us  [the longest x1 5.86 us: layers(): call(second_local_kernel, [SMEM, SMEM] + [ANY] * 17, [ANY] * 7, [hf, nf,...]
    gather x12 -> x0, local copies, waits for them, and re-layouts: 17.8 us -> none  [the longest x3 7.03 us: apply_layer(): jnp.take(from_sender, edge_src, axis=0)]
    all_to_all x3 -> x2, waiting for transfers between devices: 25.6 us -> 8.41 us  [halo_exchange(): lax.all_to_all(m.reshape(peers, -1, 128), 'dom', split_axis=0, concat_axi...]
    ppermute x2 -> x8, waiting for transfers between devices: 8.19 us -> 1.83 us  [swap(): return lax.ppermute(x, 'section', [(0, 1), (1, 0)])]
    ppermute x2 -> x8, starting transfers between devices: 2.58 us -> 8.94 us  [swap(): return lax.ppermute(x, 'section', [(0, 1), (1, 0)])]
    select_n x10 -> x0, other arithmetic: 5.02 us -> none  [the longest x4 3.9 us: apply_layer(): outgoing = jnp.take(node_lat, send_rows, axis=0)]
    all_to_all x3 -> x2, starting transfers between devices: 29.1 us -> 24.9 us  [halo_exchange(): lax.all_to_all(m.reshape(peers, -1, 128), 'dom', split_axis=0, concat_axi...]
  transfers between devices with their start and end apart: 5 -> 10, of which waited for: 5 -> 5; matrix products, arithmetic and copies ran while one was open for 10% -> 1% of each run, Pallas kernels for 0% -> 25%
where the time goes in v1:
time: 72.9 us; the launch traced here: 72.5 us
  starting transfers between devices  33.9 us (47%)
  Pallas kernels  25 us (34%)
  waiting for transfers between devices  10.2 us (14%)
  between operations  1.53 us (2%)
  local copies, waits for them, and re-layouts  1.17 us (2%)
  other arithmetic  0.75 us (1%)
    all_to_all x2, starting transfers between devices, halo_exchange(): lax.all_to_all(m.reshape(peers, -1, 128), 'dom', split_axis=0, concat_axi...  24.9 us
    ppermute x8, starting transfers between devices, swap(): return lax.ppermute(x, 'section', [(0, 1), (1, 0)])  8.94 us
    all_to_all x2, waiting for transfers between devices, halo_exchange(): lax.all_to_all(m.reshape(peers, -1, 128), 'dom', split_axis=0, concat_axi...  8.41 us
    pallas_call x1, Pallas kernels, layers(): call(second_local_kernel, [SMEM, SMEM] + [ANY] * 17, [ANY] * 7, [hf, nf,...  5.86 us
    pallas_call x1, Pallas kernels, layers(): call(functools.partial(first_local_kernel, peers), [SMEM, SMEM] + [ANY] *...  5.41 us
    pallas_call x1, Pallas kernels, layers(): call(functools.partial(last_finish_kernel, peers), [SMEM] + [ANY] * 22, [...  4.97 us
    pallas_call x1, Pallas kernels, layers(): call(functools.partial(first_finish_kernel, peers), [SMEM] + [ANY] * 19,...  4.92 us
    pallas_call x1, Pallas kernels, layers(): call(functools.partial(select_kernel, peers), [SMEM, ANY, ANY], ANY, msg,...  1.97 us
  transfers between devices with their start and end apart: 10, of which 5 were waited for; matrix products, arithmetic and copies ran while one was open for 1% of the time, Pallas kernels for 25%

profile of v1, /device:TPU:1, one launch (start us, length us, event | category | flops | bytes accessed | tf_op | source)
XLA Modules:
  0.0 72.5 jit_solution(9789771249226176041)
XLA Ops:
  0.6 3.3 %collective-permute-start = (bf16[1,3,512,512]{3,2,1,0:T(8,128)(2,1)}, bf16[1,3,512,512]{3,2,1,0:T(8,128)(2,1)}, u32[]{:S(2)}, u32[]{:S(2)}) collective-permute-start(bf16[1,3,512,512]{3,2,1,0:T(8,128)(2,1)} %ew1.7), channel_id=1, source_target_pairs={{0,128},{128,0},{1,129},{129,1},{2,130},{130,2},{3,131},{131,3},{4... | collective-permute-start | bytes 4718600 | tf_op jit(solution)/shard_map/ppermute | solution.py:338
  3.9 0.1 collective-permute-start.2
  4.0 0.4 collective-permute-start.1
  4.4 0.1 collective-permute-start.3
  4.5 2.0 %shard_map.149 = bf16[1024,128]{1,0:T(8,128)(2,1)} custom-call(s32[1]{0:T(128)} %bitcast.sec, s32[2,128]{1,0:T(2,128)} %bitcast.14, bf16[2,256,512]{2,1,0:T(8,128)(2,1)} %nfeats.1), custom_call_target="tpu_custom_call" | custom-call | flops 100000000 | bytes 1000000 | tf_op jit(solution)/shard_map/pallas_call | solution.py:340
  6.5 14.3 %all-to-all-start = ((bf16[128,8,128]{2,1,0:T(8,128)(2,1)}), bf16[128,8,128]{2,1,0:T(8,128)(2,1)}, u32[]{:S(2)}, u32[]{:S(2)}) async-start(bf16[128,8,128]{2,1,0:T(8,128)(2,1)} %bitcast.8), calls=%async_computation | async-start | bytes 524288 | tf_op jit(solution)/shard_map/all_to_all | solution.py:334
  20.9 0.8 %pad_maximum_fusion.vo_h = bf16[4,512]{1,0:T(4,128)(2,1)S(1)} fusion(bf16[1,512]{1,0:T(2,128)(2,1)} %param.27, bf16[1,512]{1,0:T(2,128)(2,1)} %param.25, bf16[1,512]{1,0:T(2,128)(2,1)} %param.23, bf16[1,512]{1,0:T(2,128)(2,1)} %param.21), kind=kLoop, calls=%fused_computation | loop fusion | flops 16384 | bytes 8192 | tf_op jit(solution)/shard_map/concatenate | solution.py:349
  21.6 0.0 copy-start
  21.6 0.6 copy-done
  22.2 0.7 collective-permute-start.4
  23.6 0.2 collective-permute-done.4.vx_h
  23.7 0.0 copy-start.1
  23.7 0.6 copy-done.1
  24.3 0.0 collective-permute-done.1.xew2
  24.3 0.0 collective-permute-done.3.xnw2
  24.3 0.0 collective-permute-done.2.xnw1
  24.3 0.0 collective-permute-done.xew1
  24.3 5.4 %shard_map.150 = (f32[256,512]{1,0:T(8,128)}, f32[256,512]{1,0:T(8,128)}, f32[256,512]{1,0:T(8,128)}, bf16[256,512]{1,0:T(8,128)(2,1)}, bf16[256,512]{1,0:T(8,12...) custom-call(s32[1]{0:T(128)} %bitcast.sec, ...), custom_call_target="tpu_custom_call" | custom-call | flops 2000000000 | bytes 10000000 | tf_op jit(solution)/shard_map/pallas_call | solution.py:353
  29.8 3.6 %all-to-all-done = bf16[128,8,128]{2,1,0:T(8,128)(2,1)} async-done(((bf16[128,8,128]{2,1,0:T(8,128)(2,1)}), bf16[128,8,128]{2,1,0:T(8,128)(2,1)}, u32[]{:S(2)}, u32[]{:S(2)}) %all-to-all-start) | async-done | bytes 262176 | tf_op jit(solution)/shard_map/all_to_all | solution.py:334
  33.4 4.9 %shard_map.151 = (bf16[1024,128]{1,0:T(8,128)(2,1)}, bf16[256,512]{1,0:T(8,128)(2,1)}, bf16[256,512]{1,0:T(8,128)(2,1)}) custom-call(s32[1]{0:T(128)} %bitcast.sec, bf16[1024,128]{1,0:T(8,128)(2,1)} %bitcast.3.msg_h, f32[256,512]{1,0:T(8,128)} %get-tuple-element.26.pre_q_h, bf16[4,512]{1,0:T(4,128)(2,1)} %copy-done, bf16[4,512]{1,0:T(4,128)(2,1)} %copy-done.1, ...), custom_call_target="tpu_custom_call" | custom-call | flops 1000000000 | bytes 4000000 | tf_op jit(solution)/shard_map/pallas_call | solution.py:361
  38.3 10.6 %all-to-all-start.1 = ((bf16[128,8,128]{2,1,0:T(8,128)(2,1)}), bf16[128,8,128]{2,1,0:T(8,128)(2,1)}, u32[]{:S(2)}, u32[]{:S(2)}) async-start(bf16[128,8,128]{2,1,0:T(8,128)(2,1)} %bitcast.9), calls=%async_computation.1 | async-start | bytes 524288 | tf_op jit(solution)/shard_map/all_to_all | solution.py:334
  48.9 5.9 %shard_map.152 = (f32[256,512]{1,0:T(8,128)}, f32[256,512]{1,0:T(8,128)}, f32[256,512]{1,0:T(8,128)}, bf16[256,512]{1,0:T(8,128)(2,1)}, bf16[256,512]{1,0:T(8,12...) custom-call(s32[1]{0:T(128)} %bitcast.sec, s32[1]{0:T(128)S(6)} %copy.24.count, ...), custom_call_target="tpu_custom_call" | custom-call | flops 2000000000 | bytes 10000000 | tf_op jit(solution)/shard_map/pallas_call | solution.py:369
  54.8 0.9 %collective-permute-start.7 = (bf16[256,512]{1,0:T(8,128)(2,1)}, bf16[256,512]{1,0:T(8,128)(2,1)}, u32[]{:S(2)}, u32[]{:S(2)}) collective-permute-start(bf16[256,512]{1,0:T(8,128)(2,1)} %get-tuple-element.47), channel_id=1, source_target_pairs={{0,128},{128,0},{1,129},{129,1},{2,130},{130,2},{3,131},{131,3},{4... | collective-permute-start | bytes 786440 | tf_op jit(solution)/shard_map/ppermute | solution.py:338
  55.7 4.8 %all-to-all-done.1 = bf16[128,8,128]{2,1,0:T(8,128)(2,1)} async-done(((bf16[128,8,128]{2,1,0:T(8,128)(2,1)}), bf16[128,8,128]{2,1,0:T(8,128)(2,1)}, u32[]{:S(2)}, u32[]{:S(2)}) %all-to-all-start.1) | async-done | bytes 262176 | tf_op jit(solution)/shard_map/all_to_all | solution.py:334
  60.5 5.0 %shard_map.153 = (bf16[256,512]{1,0:T(8,128)(2,1)}, bf16[256,512]{1,0:T(8,128)(2,1)}, bf16[1,2,256,512]{3,2,1,0:T(8,128)(2,1)}, bf16[1,2,512,512]{3,2,1,0:T(8,128)(2,1)}) custom-call(s32[1]{0:T(128)} %bitcast.sec, bf16[1024,128]{1,0:T(8,128)(2,1)} %bitcast.7.msg_h, ...), custom_call_target="tpu_custom_call", output_to_operand_aliasing={{2}: (21, {}), {3}: (22, {})} | custom-call | flops 1000000000 | bytes 4000000 | tf_op jit(solution)/shard_map/pallas_call | solution.py:378
  65.4 3.3 %collective-permute-start.5 = (bf16[256,512]{1,0:T(8,128)(2,1)}, bf16[256,512]{1,0:T(8,128)(2,1)S(1)}, u32[]{:S(2)}, u32[]{:S(2)}) collective-permute-start(bf16[256,512]{1,0:T(8,128)(2,1)} %get-tuple-element.45), channel_id=1, source_target_pairs={{0,128},{128,0},{1,129},{129,1},{2,130},{130,2},{3,131},{131,3},{4... | collective-permute-start | bytes 786440 | tf_op jit(solution)/shard_map/ppermute | solution.py:338
  68.8 0.1 collective-permute-start.6
  68.9 0.0 collective-permute-done.7.oth_l
  68.9 1.3 %collective-permute-done.5.oth_n = bf16[256,512]{1,0:T(8,128)(2,1)S(1)} collective-permute-done((bf16[256,512]{1,0:T(8,128)(2,1)}, bf16[256,512]{1,0:T(8,128)(2,1)S(1)}, u32[]{:S(2)}, u32[]{:S(2)}) %collective-permute-start.5) | collective-permute-done | bytes 262176 | tf_op jit(solution)/shard_map/ppermute | solution.py:338
  70.1 0.4 collective-permute-done.6.oth_h
  70.5 1.8 %shard_map.154 = (bf16[1,2,256,512]{3,2,1,0:T(8,128)(2,1)}, bf16[1,2,512,512]{3,2,1,0:T(8,128)(2,1)}) custom-call(s32[1]{0:T(128)} %bitcast.sec, bf16[256,512]{1,0:T(8,128)(2,1)S(1)} %collective-permute-done.5.oth_n, bf16[256,512]{1,0:T(8,128)(2,1)S(1)} %collective-permute-done.6.oth_h, ...), custom_call_target="tpu_custom_call", output_to_operand_aliasing={{0}: (4, {}), {1}: (5, {})} | custom-call | bytes 3000000 | tf_op jit(solution)/shard_map/pallas_call | solution.py:386
Async XLA Ops:
  0.6 23.7 %collective-permute-start = (bf16[1,3,512,512]{3,2,1,0:T(8,128)(2,1)}, bf16[1,3,512,512]{3,2,1,0:T(8,128)(2,1)}, u32[]{:S(2)}, u32[]{:S(2)}) collective-permute-start(bf16[1,3,512,512]{3,2,1,0:T(8,128)(2,1)} %ew1.7), channel_id=1, source_target_pairs={{0,128},{128,0},{1,129},{129,1},{2,130},{130,2},{3,131},{131,3},{4... | collective-permute-start | bytes 4718600 | tf_op jit(solution)/shard_map/ppermute | solution.py:338
  3.9 20.4 %collective-permute-start.2 = (bf16[1,2,512,512]{3,2,1,0:T(8,128)(2,1)}, bf16[1,2,512,512]{3,2,1,0:T(8,128)(2,1)}, u32[]{:S(2)}, u32[]{:S(2)}) collective-permute-start(bf16[1,2,512,512]{3,2,1,0:T(8,128)(2,1)} %nw1.7), channel_id=1, source_target_pairs={{0,128},{128,0},{1,129},{129,1},{2,130},{130,2},{3,131},{131,3},{4... | collective-permute-start | bytes 3145736 | tf_op jit(solution)/shard_map/ppermute | solution.py:338
  4.0 20.3 %collective-permute-start.1 = (bf16[1,512,512]{2,1,0:T(8,128)(2,1)}, bf16[1,512,512]{2,1,0:T(8,128)(2,1)}, u32[]{:S(2)}, u32[]{:S(2)}) collective-permute-start(bf16[1,512,512]{2,1,0:T(8,128)(2,1)} %ew2.7), channel_id=1, source_target_pairs={{0,128},{128,0},{1,129},{129,1},{2,130},{130,2},{3,131},{131,3},{4... | collective-permute-start | bytes 1572872 | tf_op jit(solution)/shard_map/ppermute | solution.py:338
  4.4 19.9 %collective-permute-start.3 = (bf16[1,512,512]{2,1,0:T(8,128)(2,1)}, bf16[1,512,512]{2,1,0:T(8,128)(2,1)}, u32[]{:S(2)}, u32[]{:S(2)}) collective-permute-start(bf16[1,512,512]{2,1,0:T(8,128)(2,1)} %nw2.7), channel_id=1, source_target_pairs={{0,128},{128,0},{1,129},{129,1},{2,130},{130,2},{3,131},{131,3},{4... | collective-permute-start | bytes 1572872 | tf_op jit(solution)/shard_map/ppermute | solution.py:338
  6.5 26.9 %all-to-all-start = ((bf16[128,8,128]{2,1,0:T(8,128)(2,1)}), bf16[128,8,128]{2,1,0:T(8,128)(2,1)}, u32[]{:S(2)}, u32[]{:S(2)}) async-start(bf16[128,8,128]{2,1,0:T(8,128)(2,1)} %bitcast.8), calls=%async_computation | async-start | bytes 524288 | tf_op jit(solution)/shard_map/all_to_all | solution.py:334
  21.6 0.6 copy-start
  22.2 1.5 %collective-permute-start.4 = (bf16[4,512]{1,0:T(4,128)(2,1)S(1)}, bf16[4,512]{1,0:T(4,128)(2,1)S(1)}, u32[]{:S(2)}, u32[]{:S(2)}) collective-permute-start(bf16[4,512]{1,0:T(4,128)(2,1)S(1)} %pad_maximum_fusion.vo_h), channel_id=1, source_target_pairs={{0,128},{128,0},{1,129},{129,1},{2,130},{130,2},{3,131},{131,3},{4... | collective-permute-start | bytes 12296 | tf_op jit(solution)/shard_map/ppermute | solution.py:338
  23.7 0.6 copy-start.1
  38.3 22.1 %all-to-all-start.1 = ((bf16[128,8,128]{2,1,0:T(8,128)(2,1)}), bf16[128,8,128]{2,1,0:T(8,128)(2,1)}, u32[]{:S(2)}, u32[]{:S(2)}) async-start(bf16[128,8,128]{2,1,0:T(8,128)(2,1)} %bitcast.9), calls=%async_computation.1 | async-start | bytes 524288 | tf_op jit(solution)/shard_map/all_to_all | solution.py:334
  54.8 14.1 %collective-permute-start.7 = (bf16[256,512]{1,0:T(8,128)(2,1)}, bf16[256,512]{1,0:T(8,128)(2,1)}, u32[]{:S(2)}, u32[]{:S(2)}) collective-permute-start(bf16[256,512]{1,0:T(8,128)(2,1)} %get-tuple-element.47), channel_id=1, source_target_pairs={{0,128},{128,0},{1,129},{129,1},{2,130},{130,2},{3,131},{131,3},{4... | collective-permute-start | bytes 786440 | tf_op jit(solution)/shard_map/ppermute | solution.py:338
  65.4 4.7 %collective-permute-start.5 = (bf16[256,512]{1,0:T(8,128)(2,1)}, bf16[256,512]{1,0:T(8,128)(2,1)S(1)}, u32[]{:S(2)}, u32[]{:S(2)}) collective-permute-start(bf16[256,512]{1,0:T(8,128)(2,1)} %get-tuple-element.45), channel_id=1, source_target_pairs={{0,128},{128,0},{1,129},{129,1},{2,130},{130,2},{3,131},{131,3},{4... | collective-permute-start | bytes 786440 | tf_op jit(solution)/shard_map/ppermute | solution.py:338
  68.8 1.7 %collective-permute-start.6 = (bf16[256,512]{1,0:T(8,128)(2,1)}, bf16[256,512]{1,0:T(8,128)(2,1)S(1)}, u32[]{:S(2)}, u32[]{:S(2)}) collective-permute-start(bf16[256,512]{1,0:T(8,128)(2,1)} %get-tuple-element.46), channel_id=1, source_target_pairs={{0,128},{128,0},{1,129},{129,1},{2,130},{130,2},{3,131},{131,3},{4... | collective-permute-start | bytes 786440 | tf_op jit(solution)/shard_map/ppermute | solution.py:338

commit v2 on v1

--- a/solution.py
+++ b/solution.py
@@ -110,13 +110,17 @@
 FINISH = (1, 3, 5, 6)
 
 
-def select_kernel(peers, sec, idx_h, feats, msg_h, idx, lat, msg, tmp, sems):
-    c_idx, c_lat = start(((idx_h, idx), (feats.at[sec[0]], lat)), sems)
-    c_idx.wait()
+def select_kernel(peers, sec, idx_h, feats, b0_h, b1_h, b2_h, b3_h, msg_h, vec_h,
+                  idx, lat, b0, b1, b2, b3, msg, vec, tmp, sems, sem_out):
+    ins = start(((feats.at[sec[0]], lat), (idx_h, idx), (b0_h, b0), (b1_h, b1), (b2_h, b2), (b3_h, b3)), sems)
+    wait(ins[1:])
+    vec[...] = jnp.concatenate([b[...].astype(F32) for b in (b0, b1, b2, b3)], axis=0).astype(BF16)
+    c_vec, = start(((vec, vec_h),), sem_out)
     oh = send_onehot(idx[...], lat.shape[0])
-    c_lat.wait()
+    ins[0].wait()
     pack_rows(dot_ta(oh, lat[...]), msg, tmp, peers)
     wait(start(((msg, msg_h),), sems))
+    c_vec.wait()
 
 
 def local_work(count, src, dst, v, e_halo, e_local, w, vec, oh_q, outs):
@@ -252,18 +256,20 @@
 
 
 def last_finish_kernel(peers, sec, msg_h, pre_q_h, vo_h, vx_h, live_h, oh_q_h, part_h, pre_n_h, e_q_h, lat_h,
-                       perm_h, e1_h_h, ew1, ew2, nw1, nw2, xew1, xew2, xnw1, xnw2, n_in, e_in,
+                       perm_h, e1_h_h, oth_l_h, ew1, ew2, nw1, nw2, xew1, xew2, xnw1, xnw2, n_in, e_in,
                        out_n_h, out_h_h, n_out, e_out,
-                       msg, pre_q, vo, vx, live_q, oh_q, part, pre_n, e_q, lat, perm_q, e1_h, w, tmp, new_n, new_h,
-                       sem_w, sem_in, sem_out):
+                       msg, pre_q, vo, vx, live_q, oh_q, part, pre_n, e_q, lat, perm_q, e1_h, oth_l,
+                       w, tmp, new_n, new_h, sem_w, sem_in, sem_out):
     mine = sec[0] == 1
     half = e_q.shape[0]
-    hbm = (msg_h, pre_q_h, vo_h, vx_h, live_h, oh_q_h, part_h, pre_n_h, e_q_h, lat_h, perm_h, e1_h_h)
-    vmem = (msg, pre_q, vo, vx, live_q, oh_q, part, pre_n, e_q, lat, perm_q, e1_h)
+    hbm = (msg_h, pre_q_h, vo_h, vx_h, live_h, oh_q_h, part_h, pre_n_h, e_q_h, lat_h, perm_h, e1_h_h, oth_l_h)
+    vmem = (msg, pre_q, vo, vx, live_q, oh_q, part, pre_n, e_q, lat, perm_q, e1_h, oth_l)
     ins, weights = start_finish(mine, hbm, vmem, (ew1, ew2, nw1, nw2), (xew1, xew2, xnw1, xnw2), w, sem_in, sem_w)
     n, e = finish(peers, mine, vmem[:10] + (w,), tmp, weights, ins[:10])
     new_n[...] = n
     wait(ins[10:])
+    c_oth = pltpu.make_async_copy(oth_l, e_out.at[0, 1 - sec[0], pl.ds(half, half)], sem_out.at[4])
+    c_oth.start()
     new_h[...] = dot_ta(perm_q[...], e).astype(BF16)
     own_n = n_out.at[0, sec[0]]
     own_h = e_out.at[0, sec[0], pl.ds(0, half)]
@@ -278,19 +284,19 @@
 
     wait([pltpu.make_async_copy(a, b, sem_out.at[i]) for i, (a, b) in enumerate(
         ((new_n, out_n_h), (new_h, out_h_h), (lat, own_n), (e1_h, own_h)))])
-
-
-def other_out_kernel(sec, oth_n, oth_h, oth_l, n_in, e_in, n_out, e_out, sems):
+    c_oth.wait()
+
+
+def other_out_kernel(sec, oth_n, oth_h, n_in, e_in, n_out, e_out, sems):
     half = oth_h.shape[0]
     other = 1 - sec[0]
     wait(start((
         (oth_n, n_out.at[0, other]),
         (oth_h, e_out.at[0, other, pl.ds(0, half)]),
-        (oth_l, e_out.at[0, other, pl.ds(half, half)]),
     ), sems))
 
 
-def call(kernel, in_specs, out_specs, out_shapes, scratch, flops, nbytes, limit=LIMIT, **kw):
+def call(kernel, in_specs, out_specs, out_shapes, scratch, flops, nbytes, limit=LIMIT - 65536, **kw):
     return pl.pallas_call(
         kernel,
         out_shape=out_shapes,
@@ -337,16 +343,16 @@
     def swap(x):
         return lax.ppermute(x, "section", [(0, 1), (1, 0)])
 
-    rows = call(
-        functools.partial(select_kernel, peers), [SMEM, ANY, ANY], ANY, msg,
-        [vmem(idx), vmem(nb), vmem(msg), tmp, DMA(2)], 10**8, 10**6,
-    )(sec, idx, node_feats)
+    rows, vec = call(
+        functools.partial(select_kernel, peers), [SMEM] + [ANY] * 6, [ANY, ANY], [msg, shape((4, width), BF16)],
+        [vmem(idx), vmem(nb)] + [vmem(edge_b1)] * 4 + [vmem(msg), pltpu.VMEM((4, width), BF16), tmp, DMA(6), DMA(1)],
+        10**8, 10**6, limit=LIMIT,
+    )(sec, idx, node_feats, edge_b1, edge_gain, node_b1, node_gain)
     halo = halo_exchange(rows)
     own_w = (edge_w1, edge_w2, node_w1, node_w2)
     oth_w = []
     for x in own_w:
         oth_w.append(swap(x))
-    vec = jnp.concatenate([edge_b1, edge_gain, node_b1, node_gain], axis=0)
     oth_vec = swap(vec)
 
     res = [hf, nf, nf, hb, nb, hb, onehot, onehot, onehot, live]
@@ -374,17 +380,17 @@
     )(sec, edge_count, src, dst, *args, *own_w, *oth_w, vec, oth_vec)
     oth_l = swap(out_l)
 
-    args = (halo, pre_q, vec, oth_vec, live_q, oh_q, part, pre_n, e1_q, n1, perm_q, e1_h)
+    args = (halo, pre_q, vec, oth_vec, live_q, oh_q, part, pre_n, e1_q, n1, perm_q, e1_h, oth_l)
     out_n, out_h, n_out, e_out = call(
-        functools.partial(last_finish_kernel, peers), [SMEM] + [ANY] * 22, [ANY] * 4, [nb, hb] + outs,
-        [vmem(x) for x in args] + [wts(4), tmp, vmem(nb), vmem(hb), DMA(4), DMA(12), DMA(4)],
-        10**9, 4 * 10**6, input_output_aliases={21: 2, 22: 3},
+        functools.partial(last_finish_kernel, peers), [SMEM] + [ANY] * 23, [ANY] * 4, [nb, hb] + outs,
+        [vmem(x) for x in args] + [wts(4), tmp, vmem(nb), vmem(hb), DMA(4), DMA(13), DMA(5)],
+        10**9, 4 * 10**6, input_output_aliases={22: 2, 23: 3},
     )(sec, *args, *own_w, *oth_w, n_out, e_out)
     oth_h = swap(out_h)
     oth_n = swap(out_n)
 
-    return call(other_out_kernel, [SMEM] + [VMEM] * 3 + [ANY, ANY], [ANY, ANY], outs, [DMA(3)], 0, 3 * 10**6,
-                limit=1024 * 1024, input_output_aliases={4: 0, 5: 1})(sec, oth_n, oth_h, oth_l, n_out, e_out)
+    return call(other_out_kernel, [SMEM] + [VMEM] * 2 + [ANY, ANY], [ANY, ANY], outs, [DMA(2)], 0, 3 * 10**6,
+                limit=1024 * 1024, input_output_aliases={3: 0, 4: 1})(sec, oth_n, oth_h, n_out, e_out)
 
 
 def solution(mesh):

time: 72.9 us -> 70.8 us (0.971)
  waiting for transfers between devices: 10.2 us -> 11.5 us
  Pallas kernels: 25 us -> 24 us
  starting transfers between devices: 33.9 us -> 32.9 us
  other arithmetic: 0.75 us -> 0 us
    ppermute x8, waiting for transfers between devices: 1.83 us -> 3.54 us  [swap(): return lax.ppermute(x, 'section', [(0, 1), (1, 0)])]
    all_to_all x2, starting transfers between devices: 24.9 us -> 23.8 us  [halo_exchange(): lax.all_to_all(m.reshape(peers, -1, 128), 'dom', split_axis=0, concat_axi...]
    pallas_call x3, Pallas kernels: 8.79 us -> 7.82 us  [the longest x1 5.02 us: layers(): call(functools.partial(last_finish_kernel, peers), [SMEM] + [ANY] * 23, [...]
    concatenate x1 -> x0, other arithmetic: 0.75 us -> none  [layers(): vec = jnp.concatenate([edge_b1, edge_gain, node_b1, node_gain], axis=0)]
  transfers between devices with their start and end apart: 10 -> 10, of which waited for: 5 -> 6; matrix products, arithmetic and copies ran while one was open for 1% -> 0% of each run, Pallas kernels for 25% -> 19%
where the time goes in v2:
time: 70.8 us; the launch traced here: 70.5 us
  starting transfers between devices  32.9 us (46%)
  Pallas kernels  24 us (34%)
  waiting for transfers between devices  11.5 us (16%)
  between operations  1.52 us (2%)
    all_to_all x2, starting transfers between devices, halo_exchange(): lax.all_to_all(m.reshape(peers, -1, 128), 'dom', split_axis=0, concat_axi...  23.8 us
    ppermute x8, starting transfers between devices, swap(): return lax.ppermute(x, 'section', [(0, 1), (1, 0)])  9.06 us
    all_to_all x2, waiting for transfers between devices, halo_exchange(): lax.all_to_all(m.reshape(peers, -1, 128), 'dom', split_axis=0, concat_axi...  7.99 us
    pallas_call x1, Pallas kernels, layers(): call(second_local_kernel, [SMEM, SMEM] + [ANY] * 17, [ANY] * 7, [hf, nf,...  5.86 us
    pallas_call x1, Pallas kernels, layers(): call(functools.partial(first_local_kernel, peers), [SMEM, SMEM] + [ANY] *...  5.4 us
    pallas_call x1, Pallas kernels, layers(): call(functools.partial(last_finish_kernel, peers), [SMEM] + [ANY] * 23, [...  5.02 us
    pallas_call x1, Pallas kernels, layers(): call(functools.partial(first_finish_kernel, peers), [SMEM] + [ANY] * 19,...  4.91 us
    ppermute x8, waiting for transfers between devices, swap(): return lax.ppermute(x, 'section', [(0, 1), (1, 0)])  3.54 us
  transfers between devices with their start and end apart: 10, of which 6 were waited for; matrix products, arithmetic and copies ran while one was open for 0% of the time, Pallas kernels for 19%

profile of v2, /device:TPU:1, one launch (start us, length us, event | category | flops | bytes accessed | tf_op | source)
XLA Modules:
  0.0 70.5 jit_solution(798329375617137442)
XLA Ops:
  0.6 3.3 %collective-permute-start = (bf16[1,3,512,512]{3,2,1,0:T(8,128)(2,1)}, bf16[1,3,512,512]{3,2,1,0:T(8,128)(2,1)}, u32[]{:S(2)}, u32[]{:S(2)}) collective-permute-start(bf16[1,3,512,512]{3,2,1,0:T(8,128)(2,1)} %ew1.7), channel_id=1, source_target_pairs={{0,128},{128,0},{1,129},{129,1},{2,130},{130,2},{3,131},{131,3},{4... | collective-permute-start | bytes 4718600 | tf_op jit(solution)/shard_map/ppermute | solution.py:344
  3.9 0.1 collective-permute-start.2
  4.0 0.4 collective-permute-start.1
  4.4 0.1 collective-permute-start.3
  4.5 2.0 %shard_map.149 = (bf16[1024,128]{1,0:T(8,128)(2,1)}, bf16[4,512]{1,0:T(4,128)(2,1)}) custom-call(s32[1]{0:T(128)} %bitcast.sec, s32[2,128]{1,0:T(2,128)} %bitcast.14, bf16[2,256,512]{2,1,0:T(8,128)(2,1)} %nfeats.1, bf16[1,512]{1,0:T(2,128)(2,1)} %b0_h.1, bf16[1,512]{1,0:T(2,128)(2,1)} %b1_h.1, bf16[1,512]{1,0:T(2,128)(2,1)} %b2_h.1, bf16[1,512]{1,0:T(2,128)(2,1)} %b3_h.1), custom_call_target="tpu_custom_call" | custom-call | flops 100000000 | bytes 1000000 | tf_op jit(solution)/shard_map/pallas_call | solution.py:346
  6.5 14.3 %all-to-all-start = ((bf16[128,8,128]{2,1,0:T(8,128)(2,1)}), bf16[128,8,128]{2,1,0:T(8,128)(2,1)}, u32[]{:S(2)}, u32[]{:S(2)}) async-start(bf16[128,8,128]{2,1,0:T(8,128)(2,1)} %bitcast.8), calls=%async_computation | async-start | bytes 524288 | tf_op jit(solution)/shard_map/all_to_all | solution.py:340
  20.9 0.8 %collective-permute-start.4 = (bf16[4,512]{1,0:T(4,128)(2,1)}, bf16[4,512]{1,0:T(4,128)(2,1)S(1)}, u32[]{:S(2)}, u32[]{:S(2)}) collective-permute-start(bf16[4,512]{1,0:T(4,128)(2,1)} %get-tuple-element.29.vo_h), channel_id=1, source_target_pairs={{0,128},{128,0},{1,129},{129,1},{2,130},{130,2},{3,131},{131,3},{4... | collective-permute-start | bytes 12296 | tf_op jit(solution)/shard_map/ppermute | solution.py:344
  22.3 0.4 collective-permute-done.4.vx_h
  22.7 0.0 copy-start
  22.7 0.0 collective-permute-done.1.xew2
  22.7 0.0 collective-permute-done.3.xnw2
  22.7 0.0 collective-permute-done.2.xnw1
  22.7 0.0 collective-permute-done.xew1
  22.7 0.6 copy-done
  23.3 5.4 %shard_map.150 = (f32[256,512]{1,0:T(8,128)}, f32[256,512]{1,0:T(8,128)}, f32[256,512]{1,0:T(8,128)}, bf16[256,512]{1,0:T(8,128)(2,1)}, bf16[256,512]{1,0:T(8,12...) custom-call(s32[1]{0:T(128)} %bitcast.sec, ...), custom_call_target="tpu_custom_call" | custom-call | flops 2000000000 | bytes 10000000 | tf_op jit(solution)/shard_map/pallas_call | solution.py:359
  28.7 4.7 %all-to-all-done = bf16[128,8,128]{2,1,0:T(8,128)(2,1)} async-done(((bf16[128,8,128]{2,1,0:T(8,128)(2,1)}), bf16[128,8,128]{2,1,0:T(8,128)(2,1)}, u32[]{:S(2)}, u32[]{:S(2)}) %all-to-all-start) | async-done | bytes 262176 | tf_op jit(solution)/shard_map/all_to_all | solution.py:340
  33.4 4.9 %shard_map.151 = (bf16[1024,128]{1,0:T(8,128)(2,1)}, bf16[256,512]{1,0:T(8,128)(2,1)}, bf16[256,512]{1,0:T(8,128)(2,1)}) custom-call(s32[1]{0:T(128)} %bitcast.sec, bf16[1024,128]{1,0:T(8,128)(2,1)} %bitcast.3.msg_h, f32[256,512]{1,0:T(8,128)} %get-tuple-element.30.pre_q_h, bf16[4,512]{1,0:T(4,128)(2,1)} %get-tuple-element.29.vo_h, bf16[4,512]{1,0:T(4,128)(2,1)} %copy-done, ...), custom_call_target="tpu_custom_call" | custom-call | flops 1000000000 | bytes 4000000 | tf_op jit(solution)/shard_map/pallas_call | solution.py:367
  38.3 9.5 %all-to-all-start.1 = ((bf16[128,8,128]{2,1,0:T(8,128)(2,1)}), bf16[128,8,128]{2,1,0:T(8,128)(2,1)}, u32[]{:S(2)}, u32[]{:S(2)}) async-start(bf16[128,8,128]{2,1,0:T(8,128)(2,1)} %bitcast.9), calls=%async_computation.1 | async-start | bytes 524288 | tf_op jit(solution)/shard_map/all_to_all | solution.py:340
  47.8 5.9 %shard_map.152 = (f32[256,512]{1,0:T(8,128)}, f32[256,512]{1,0:T(8,128)}, f32[256,512]{1,0:T(8,128)}, bf16[256,512]{1,0:T(8,128)(2,1)}, bf16[256,512]{1,0:T(8,12...) custom-call(s32[1]{0:T(128)} %bitcast.sec, s32[1]{0:T(128)S(6)} %copy.24.count, ...), custom_call_target="tpu_custom_call" | custom-call | flops 2000000000 | bytes 10000000 | tf_op jit(solution)/shard_map/pallas_call | solution.py:375
  53.7 0.9 %collective-permute-start.5 = (bf16[256,512]{1,0:T(8,128)(2,1)}, bf16[256,512]{1,0:T(8,128)(2,1)}, u32[]{:S(2)}, u32[]{:S(2)}) collective-permute-start(bf16[256,512]{1,0:T(8,128)(2,1)} %get-tuple-element.47), channel_id=1, source_target_pairs={{0,128},{128,0},{1,129},{129,1},{2,130},{130,2},{3,131},{131,3},{4... | collective-permute-start | bytes 786440 | tf_op jit(solution)/shard_map/ppermute | solution.py:344
  54.6 1.5 %collective-permute-done.5.oth_l_h = bf16[256,512]{1,0:T(8,128)(2,1)} collective-permute-done((bf16[256,512]{1,0:T(8,128)(2,1)}, bf16[256,512]{1,0:T(8,128)(2,1)}, u32[]{:S(2)}, u32[]{:S(2)}) %collective-permute-start.5) | collective-permute-done | bytes 262176 | tf_op jit(solution)/shard_map/ppermute | solution.py:344
  56.1 3.3 %all-to-all-done.1 = bf16[128,8,128]{2,1,0:T(8,128)(2,1)} async-done(((bf16[128,8,128]{2,1,0:T(8,128)(2,1)}), bf16[128,8,128]{2,1,0:T(8,128)(2,1)}, u32[]{:S(2)}, u32[]{:S(2)}) %all-to-all-start.1) | async-done | bytes 262176 | tf_op jit(solution)/shard_map/all_to_all | solution.py:340
  59.4 5.0 %shard_map.153 = (bf16[256,512]{1,0:T(8,128)(2,1)}, bf16[256,512]{1,0:T(8,128)(2,1)}, bf16[1,2,256,512]{3,2,1,0:T(8,128)(2,1)}, bf16[1,2,512,512]{3,2,1,0:T(8,128)(2,1)}) custom-call(s32[1]{0:T(128)} %bitcast.sec, bf16[1024,128]{1,0:T(8,128)(2,1)} %bitcast.7.msg_h, ...), custom_call_target="tpu_custom_call", output_to_operand_aliasing={{2}: (22, {}), {3}: (23, {})} | custom-call | flops 1000000000 | bytes 4000000 | tf_op jit(solution)/shard_map/pallas_call | solution.py:384
  64.4 3.4 %collective-permute-start.6 = (bf16[256,512]{1,0:T(8,128)(2,1)}, bf16[256,512]{1,0:T(8,128)(2,1)S(1)}, u32[]{:S(2)}, u32[]{:S(2)}) collective-permute-start(bf16[256,512]{1,0:T(8,128)(2,1)} %get-tuple-element.50), channel_id=1, source_target_pairs={{0,128},{128,0},{1,129},{129,1},{2,130},{130,2},{3,131},{131,3},{4... | collective-permute-start | bytes 786440 | tf_op jit(solution)/shard_map/ppermute | solution.py:344
  67.8 0.1 collective-permute-start.7
  67.9 1.3 %collective-permute-done.6.oth_n = bf16[256,512]{1,0:T(8,128)(2,1)S(1)} collective-permute-done((bf16[256,512]{1,0:T(8,128)(2,1)}, bf16[256,512]{1,0:T(8,128)(2,1)S(1)}, u32[]{:S(2)}, u32[]{:S(2)}) %collective-permute-start.6) | collective-permute-done | bytes 262176 | tf_op jit(solution)/shard_map/ppermute | solution.py:344
  69.2 0.4 collective-permute-done.7.oth_h
  69.5 0.8 %shard_map.154 = (bf16[1,2,256,512]{3,2,1,0:T(8,128)(2,1)}, bf16[1,2,512,512]{3,2,1,0:T(8,128)(2,1)}) custom-call(s32[1]{0:T(128)} %bitcast.sec, bf16[256,512]{1,0:T(8,128)(2,1)S(1)} %collective-permute-done.6.oth_n, bf16[256,512]{1,0:T(8,128)(2,1)S(1)} %collective-permute-done.7.oth_h, ...), custom_call_target="tpu_custom_call", output_to_operand_aliasing={{0}: (3, {}), {1}: (4, {})} | custom-call | bytes 3000000 | tf_op jit(solution)/shard_map/pallas_call | solution.py:392
Async XLA Ops:
  0.6 22.1 %collective-permute-start = (bf16[1,3,512,512]{3,2,1,0:T(8,128)(2,1)}, bf16[1,3,512,512]{3,2,1,0:T(8,128)(2,1)}, u32[]{:S(2)}, u32[]{:S(2)}) collective-permute-start(bf16[1,3,512,512]{3,2,1,0:T(8,128)(2,1)} %ew1.7), channel_id=1, source_target_pairs={{0,128},{128,0},{1,129},{129,1},{2,130},{130,2},{3,131},{131,3},{4... | collective-permute-start | bytes 4718600 | tf_op jit(solution)/shard_map/ppermute | solution.py:344
  3.9 18.8 %collective-permute-start.2 = (bf16[1,2,512,512]{3,2,1,0:T(8,128)(2,1)}, bf16[1,2,512,512]{3,2,1,0:T(8,128)(2,1)}, u32[]{:S(2)}, u32[]{:S(2)}) collective-permute-start(bf16[1,2,512,512]{3,2,1,0:T(8,128)(2,1)} %nw1.7), channel_id=1, source_target_pairs={{0,128},{128,0},{1,129},{129,1},{2,130},{130,2},{3,131},{131,3},{4... | collective-permute-start | bytes 3145736 | tf_op jit(solution)/shard_map/ppermute | solution.py:344
  4.0 18.7 %collective-permute-start.1 = (bf16[1,512,512]{2,1,0:T(8,128)(2,1)}, bf16[1,512,512]{2,1,0:T(8,128)(2,1)}, u32[]{:S(2)}, u32[]{:S(2)}) collective-permute-start(bf16[1,512,512]{2,1,0:T(8,128)(2,1)} %ew2.7), channel_id=1, source_target_pairs={{0,128},{128,0},{1,129},{129,1},{2,130},{130,2},{3,131},{131,3},{4... | collective-permute-start | bytes 1572872 | tf_op jit(solution)/shard_map/ppermute | solution.py:344
  4.4 18.3 %collective-permute-start.3 = (bf16[1,512,512]{2,1,0:T(8,128)(2,1)}, bf16[1,512,512]{2,1,0:T(8,128)(2,1)}, u32[]{:S(2)}, u32[]{:S(2)}) collective-permute-start(bf16[1,512,512]{2,1,0:T(8,128)(2,1)} %nw2.7), channel_id=1, source_target_pairs={{0,128},{128,0},{1,129},{129,1},{2,130},{130,2},{3,131},{131,3},{4... | collective-permute-start | bytes 1572872 | tf_op jit(solution)/shard_map/ppermute | solution.py:344
  6.5 26.9 %all-to-all-start = ((bf16[128,8,128]{2,1,0:T(8,128)(2,1)}), bf16[128,8,128]{2,1,0:T(8,128)(2,1)}, u32[]{:S(2)}, u32[]{:S(2)}) async-start(bf16[128,8,128]{2,1,0:T(8,128)(2,1)} %bitcast.8), calls=%async_computation | async-start | bytes 524288 | tf_op jit(solution)/shard_map/all_to_all | solution.py:340
  20.9 1.8 %collective-permute-start.4 = (bf16[4,512]{1,0:T(4,128)(2,1)}, bf16[4,512]{1,0:T(4,128)(2,1)S(1)}, u32[]{:S(2)}, u32[]{:S(2)}) collective-permute-start(bf16[4,512]{1,0:T(4,128)(2,1)} %get-tuple-element.29.vo_h), channel_id=1, source_target_pairs={{0,128},{128,0},{1,129},{129,1},{2,130},{130,2},{3,131},{131,3},{4... | collective-permute-start | bytes 12296 | tf_op jit(solution)/shard_map/ppermute | solution.py:344
  22.7 0.6 copy-start
  38.3 21.1 %all-to-all-start.1 = ((bf16[128,8,128]{2,1,0:T(8,128)(2,1)}), bf16[128,8,128]{2,1,0:T(8,128)(2,1)}, u32[]{:S(2)}, u32[]{:S(2)}) async-start(bf16[128,8,128]{2,1,0:T(8,128)(2,1)} %bitcast.9), calls=%async_computation.1 | async-start | bytes 524288 | tf_op jit(solution)/shard_map/all_to_all | solution.py:340
  53.7 2.4 %collective-permute-start.5 = (bf16[256,512]{1,0:T(8,128)(2,1)}, bf16[256,512]{1,0:T(8,128)(2,1)}, u32[]{:S(2)}, u32[]{:S(2)}) collective-permute-start(bf16[256,512]{1,0:T(8,128)(2,1)} %get-tuple-element.47), channel_id=1, source_target_pairs={{0,128},{128,0},{1,129},{129,1},{2,130},{130,2},{3,131},{131,3},{4... | collective-permute-start | bytes 786440 | tf_op jit(solution)/shard_map/ppermute | solution.py:344
  64.4 4.7 %collective-permute-start.6 = (bf16[256,512]{1,0:T(8,128)(2,1)}, bf16[256,512]{1,0:T(8,128)(2,1)S(1)}, u32[]{:S(2)}, u32[]{:S(2)}) collective-permute-start(bf16[256,512]{1,0:T(8,128)(2,1)} %get-tuple-element.50), channel_id=1, source_target_pairs={{0,128},{128,0},{1,129},{129,1},{2,130},{130,2},{3,131},{131,3},{4... | collective-permute-start | bytes 786440 | tf_op jit(solution)/shard_map/ppermute | solution.py:344
  67.8 1.7 %collective-permute-start.7 = (bf16[256,512]{1,0:T(8,128)(2,1)}, bf16[256,512]{1,0:T(8,128)(2,1)S(1)}, u32[]{:S(2)}, u32[]{:S(2)}) collective-permute-start(bf16[256,512]{1,0:T(8,128)(2,1)} %get-tuple-element.51), channel_id=1, source_target_pairs={{0,128},{128,0},{1,129},{129,1},{2,130},{130,2},{3,131},{131,3},{4... | collective-permute-start | bytes 786440 | tf_op jit(solution)/shard_map/ppermute | solution.py:344

commit v3 on v2

--- a/solution.py
+++ b/solution.py
@@ -90,8 +90,9 @@
 
 
 def matrices(refs):
-    ew1, ew2, nw1, nw2 = refs
-    return ew1.at[0, 0], ew1.at[0, 1], ew1.at[0, 2], ew2.at[0], nw1.at[0, 0], nw1.at[0, 1], nw2.at[0]
+    ew1, ew2, nw1 = refs[:3]
+    return (ew1.at[0, 0], ew1.at[0, 1], ew1.at[0, 2], ew2.at[0], nw1.at[0, 0], nw1.at[0, 1]) + tuple(
+        r.at[0] for r in refs[3:])
 
 
 def fetch_weights(mine, own, oth, which, w, sems):
@@ -147,8 +148,8 @@
     return jnp.where(mine, vec_own[...].astype(F32), vec_oth[...].astype(F32))
 
 
-def first_local_kernel(peers, sec, count, src_h, dst_h, idx_h, nfeats, efeats, ew1, ew2, nw1, nw2,
-                       xew1, xew2, xnw1, xnw2, vo_h, vx_h,
+def first_local_kernel(peers, sec, count, src_h, dst_h, idx_h, nfeats, efeats, ew1, ew2, nw1,
+                       xew1, xew2, xnw1, vo_h, vx_h,
                        pre_q_h, part_h, pre_n_h, e1_loc_h, lat_h, e_q_h, oh_q_h, oh_s_h, perm_h, live_h,
                        src, dst, idx, vo, vx, lat, e, w, pre_q, part, pre_n, e1_loc, e_q, oh_q, oh_s, perm_q, live_q,
                        sem_w, sem_in, sem_out):
@@ -157,7 +158,7 @@
     mine = sec[0] == 0
     ins = start(((src_h, src), (dst_h, dst), (idx_h, idx), (efeats.at[sec[0]], e), (nfeats.at[sec[0]], lat),
                  (vo_h, vo), (vx_h, vx)), sem_in)
-    weights = fetch_weights(mine, (ew1, ew2, nw1, nw2), (xew1, xew2, xnw1, xnw2), LOCAL, w, sem_w)
+    weights = fetch_weights(mine, (ew1, ew2, nw1), (xew1, xew2, xnw1), LOCAL, w, sem_w)
     wait(ins)
     oh_s[...] = send_onehot(idx[...], nodes)
     perm = pick_onehot(src[:, :half], arrival_ids(half, peers, nodes))
@@ -177,16 +178,16 @@
                 (oh_q, oh_q_h), (oh_s, oh_s_h), (perm_q, perm_h), (live_q, live_h)), sem_out))
 
 
-def second_local_kernel(sec, count, src_h, dst_h, lat_h, e_q_h, e_loc_h, oh_q_h, perm_h, ew1, ew2, nw1, nw2,
-                        xew1, xew2, xnw1, xnw2, vo_h, vx_h,
-                        pre_q_h, part_h, pre_n_h, e1_h_h, out_l_h, n_out, e_out,
+def second_local_kernel(sec, count, src_h, dst_h, lat_h, e_q_h, e_loc_h, oh_q_h, perm_h, ew1, ew2, nw1,
+                        xew1, xew2, xnw1, vo_h, vx_h,
+                        pre_q_h, part_h, pre_n_h, e1_h_h, out_l_h, e_out,
                         src, dst, vo, vx, lat, e_q, e_loc, oh_q, perm_q, w, pre_q, part, pre_n, e1_h, own_l, out_l,
                         sem_w, sem_in, sem_out):
     half = src.shape[1] // 2
     mine = sec[0] == 1
     ins = start(((src_h, src), (dst_h, dst), (lat_h, lat), (e_q_h, e_q), (e_loc_h, e_loc), (oh_q_h, oh_q),
                  (perm_h, perm_q), (vo_h, vo), (vx_h, vx)), sem_in)
-    weights = fetch_weights(mine, (ew1, ew2, nw1, nw2), (xew1, xew2, xnw1, xnw2), LOCAL, w, sem_w)
+    weights = fetch_weights(mine, (ew1, ew2, nw1), (xew1, xew2, xnw1), LOCAL, w, sem_w)
     wait(ins)
     eq = e_q[...]
     e1_h[...] = dot_ta(perm_q[...], eq).astype(BF16)
@@ -209,90 +210,111 @@
                 (own_l, e_out.at[0, sec[0], pl.ds(half, half)])), sem_out))
 
 
-def finish(peers, mine, refs, tmp, weights, ins):
-    msg, pre_q, vo, vx, live_q, oh_q, part, pre_n, e_q, lat, w = refs
-    c_msg, c_pre, c_vo, c_vx, c_live, c_ohq, c_part, c_pren, c_eq, c_lat = ins
-    c_msg.wait()
+def finish(peers, mine, refs, waits, on_edges):
+    msg, pre_q, vo, vx, live_q, oh_q, part, e_q, pre_n, lat, w, tmp = refs
+    waits[0]()
     halo = unpack_rows(msg, tmp, e_q.shape[0], e_q.shape[1], peers)
-    wait((c_pre, c_vo, c_vx, weights[0]))
+    waits[1]()
     vec = pick_vec(mine, vo, vx)
     h = pre_q[...] + dot(halo, w[0])
     hid = silu(h).astype(BF16)
-    wait((weights[1], c_live, c_ohq, c_part, c_eq))
+    waits[2]()
     y = centre(dot(hid, w[1])) * vec[1:2]
     upd = jnp.where(live_q[:, 0:1] > 0.5, y, 0.0)
     incoming = (part[...] + dot(oh_q[...], upd.astype(BF16))).astype(BF16)
-    new_e = (e_q[...].astype(F32) + upd).astype(BF16)
-    wait((weights[2], weights[3], c_pren, c_lat))
+    on_edges((e_q[...].astype(F32) + upd).astype(BF16))
     hn = silu(pre_n[...] + dot(incoming, w[2])).astype(BF16)
     yn = centre(dot(hn, w[3])) * vec[3:4]
-    new_n = (lat[...].astype(F32) + yn).astype(BF16)
-    return new_n, new_e
+    return (lat[...].astype(F32) + yn).astype(BF16)
 
 
 def start_finish(mine, hbm, vmem, own, oth, w, sem_in, sem_w):
-    first = start(((hbm[0], vmem[0]),), sem_in)
-    weights = fetch_weights(mine, own, oth, FINISH, w, sem_w)
-    rest = [pltpu.make_async_copy(a, b, sem_in.at[i + 1]) for i, (a, b) in enumerate(zip(hbm[1:], vmem[1:]))]
-    for c in rest:
-        c.start()
-    return first + rest, weights
-
-
-def first_finish_kernel(peers, sec, msg_h, pre_q_h, vo_h, vx_h, live_h, oh_q_h, part_h, pre_n_h, e_q_h, lat_h, oh_s_h,
+    def copies(refs):
+        m = [matrices(refs)[k] for k in FINISH]
+        data = [pltpu.make_async_copy(a, b, sem_in.at[i]) for i, (a, b) in enumerate(zip(hbm, vmem))]
+        mats = [pltpu.make_async_copy(a, w.at[i], sem_w.at[i]) for i, a in enumerate(m)]
+        return data[:1], [mats[0]] + data[1:4], [mats[1]] + data[4:8] + mats[2:] + data[8:]
+
+    def go(refs):
+        for group in copies(refs):
+            for c in group:
+                c.start()
+
+    @pl.when(mine)
+    def _():
+        go(own)
+
+    @pl.when(jnp.logical_not(mine))
+    def _():
+        go(oth)
+
+    return [functools.partial(wait, group) for group in copies(own)]
+
+
+def first_finish_kernel(peers, sec, msg_h, pre_q_h, vo_h, vx_h, live_h, oh_q_h, part_h, e_q_h, pre_n_h, lat_h, oh_s_h,
                         ew1, ew2, nw1, nw2, xew1, xew2, xnw1, xnw2, out_msg_h, new_n_h, new_e_h,
-                        msg, pre_q, vo, vx, live_q, oh_q, part, pre_n, e_q, lat, oh_s, w, tmp, out_msg, new_n, new_e,
+                        msg, pre_q, vo, vx, live_q, oh_q, part, e_q, pre_n, lat, oh_s, w, tmp, out_msg, new_n, new_e,
                         sem_w, sem_in, sem_out):
     mine = sec[0] == 0
-    hbm = (msg_h, pre_q_h, vo_h, vx_h, live_h, oh_q_h, part_h, pre_n_h, e_q_h, lat_h, oh_s_h)
-    vmem = (msg, pre_q, vo, vx, live_q, oh_q, part, pre_n, e_q, lat, oh_s)
-    ins, weights = start_finish(mine, hbm, vmem, (ew1, ew2, nw1, nw2), (xew1, xew2, xnw1, xnw2), w, sem_in, sem_w)
-    n, e = finish(peers, mine, vmem[:10] + (w,), tmp, weights, ins[:10])
+    hbm = (msg_h, pre_q_h, vo_h, vx_h, live_h, oh_q_h, part_h, e_q_h, pre_n_h, lat_h, oh_s_h)
+    vmem = (msg, pre_q, vo, vx, live_q, oh_q, part, e_q, pre_n, lat, oh_s)
+    waits = start_finish(mine, hbm, vmem, (ew1, ew2, nw1, nw2), (xew1, xew2, xnw1, xnw2), w, sem_in, sem_w)
+    c_msg, c_n, c_e = [pltpu.make_async_copy(a, b, sem_out.at[i]) for i, (a, b) in enumerate(
+        ((out_msg, out_msg_h), (new_n, new_n_h), (new_e, new_e_h)))]
+
+    def on_edges(e):
+        new_e[...] = e
+        c_e.start()
+
+    n = finish(peers, mine, vmem[:10] + (w, tmp), waits, on_edges)
     new_n[...] = n
-    new_e[...] = e
-    ins[10].wait()
     pack_rows(dot_ta(oh_s[...], n), out_msg, tmp, peers)
-    wait(start(((out_msg, out_msg_h), (new_n, new_n_h), (new_e, new_e_h)), sem_out))
-
-
-def last_finish_kernel(peers, sec, msg_h, pre_q_h, vo_h, vx_h, live_h, oh_q_h, part_h, pre_n_h, e_q_h, lat_h,
-                       perm_h, e1_h_h, oth_l_h, ew1, ew2, nw1, nw2, xew1, xew2, xnw1, xnw2, n_in, e_in,
-                       out_n_h, out_h_h, n_out, e_out,
-                       msg, pre_q, vo, vx, live_q, oh_q, part, pre_n, e_q, lat, perm_q, e1_h, oth_l,
-                       w, tmp, new_n, new_h, sem_w, sem_in, sem_out):
+    c_msg.start()
+    c_n.start()
+    wait((c_e, c_msg, c_n))
+
+
+def last_finish_kernel(peers, sec, msg_h, pre_q_h, vo_h, vx_h, live_h, oh_q_h, part_h, e_q_h, pre_n_h, lat_h,
+                       perm_h, e1_h_h, oth_l_h, ew1, ew2, nw1, nw2, xew1, xew2, xnw1, xnw2, e_in,
+                       cross, n_out, e_out,
+                       msg, pre_q, vo, vx, live_q, oh_q, part, e_q, pre_n, lat, perm_q, e1_h, oth_l,
+                       w, tmp, own_h, out_h, own_n, out_n, sem_w, sem_in, sem_out):
     mine = sec[0] == 1
-    half = e_q.shape[0]
-    hbm = (msg_h, pre_q_h, vo_h, vx_h, live_h, oh_q_h, part_h, pre_n_h, e_q_h, lat_h, perm_h, e1_h_h, oth_l_h)
-    vmem = (msg, pre_q, vo, vx, live_q, oh_q, part, pre_n, e_q, lat, perm_q, e1_h, oth_l)
-    ins, weights = start_finish(mine, hbm, vmem, (ew1, ew2, nw1, nw2), (xew1, xew2, xnw1, xnw2), w, sem_in, sem_w)
-    n, e = finish(peers, mine, vmem[:10] + (w,), tmp, weights, ins[:10])
-    new_n[...] = n
-    wait(ins[10:])
-    c_oth = pltpu.make_async_copy(oth_l, e_out.at[0, 1 - sec[0], pl.ds(half, half)], sem_out.at[4])
-    c_oth.start()
-    new_h[...] = dot_ta(perm_q[...], e).astype(BF16)
-    own_n = n_out.at[0, sec[0]]
-    own_h = e_out.at[0, sec[0], pl.ds(0, half)]
-
-    @pl.when(mine)
-    def _():
-        start(((new_n, own_n), (new_h, own_h), (lat, out_n_h), (e1_h, out_h_h)), sem_out)
-
-    @pl.when(jnp.logical_not(mine))
-    def _():
-        start(((new_n, out_n_h), (new_h, out_h_h), (lat, own_n), (e1_h, own_h)), sem_out)
-
-    wait([pltpu.make_async_copy(a, b, sem_out.at[i]) for i, (a, b) in enumerate(
-        ((new_n, out_n_h), (new_h, out_h_h), (lat, own_n), (e1_h, own_h)))])
-    c_oth.wait()
-
-
-def other_out_kernel(sec, oth_n, oth_h, n_in, e_in, n_out, e_out, sems):
-    half = oth_h.shape[0]
+    half, nodes = e_q.shape[0], lat.shape[0]
+    hbm = (msg_h, pre_q_h, vo_h, vx_h, live_h, oh_q_h, part_h, e_q_h, pre_n_h, lat_h, perm_h, e1_h_h, oth_l_h)
+    vmem = (msg, pre_q, vo, vx, live_q, oh_q, part, e_q, pre_n, lat, perm_q, e1_h, oth_l)
+    waits = start_finish(mine, hbm, vmem, (ew1, ew2, nw1, nw2), (xew1, xew2, xnw1, xnw2), w, sem_in, sem_w)
+    writes = [pltpu.make_async_copy(a, b, sem_out.at[i]) for i, (a, b) in enumerate((
+        (out_h, cross.at[pl.ds(nodes, half)]),
+        (own_h, e_out.at[0, sec[0], pl.ds(0, half)]),
+        (oth_l, e_out.at[0, 1 - sec[0], pl.ds(half, half)]),
+        (out_n, cross.at[pl.ds(0, nodes)]),
+        (own_n, n_out.at[0, sec[0]]),
+    ))]
+
+    def on_edges(e):
+        new_h = dot_ta(perm_q[...], e)
+        old_h = e1_h[...].astype(F32)
+        out_h[...] = jnp.where(mine, old_h, new_h).astype(BF16)
+        own_h[...] = jnp.where(mine, new_h, old_h).astype(BF16)
+        for c in writes[:3]:
+            c.start()
+
+    n = finish(peers, mine, vmem[:10] + (w, tmp), waits, on_edges).astype(F32)
+    old_n = lat[...].astype(F32)
+    out_n[...] = jnp.where(mine, old_n, n).astype(BF16)
+    own_n[...] = jnp.where(mine, n, old_n).astype(BF16)
+    for c in writes[3:]:
+        c.start()
+    wait(writes)
+
+
+def other_out_kernel(sec, crossed, n_in, e_in, n_out, e_out, sems):
+    nodes, slots = n_out.shape[2], e_out.shape[2]
     other = 1 - sec[0]
     wait(start((
-        (oth_n, n_out.at[0, other]),
-        (oth_h, e_out.at[0, other, pl.ds(0, half)]),
+        (crossed.at[pl.ds(0, nodes)], n_out.at[0, other]),
+        (crossed.at[pl.ds(nodes, slots // 2)], e_out.at[0, other, pl.ds(0, slots // 2)]),
     ), sems))
 
 
@@ -357,13 +379,13 @@
 
     res = [hf, nf, nf, hb, nb, hb, onehot, onehot, onehot, live]
     pre_q, part, pre_n, e1_loc, lat, e_q, oh_q, oh_s, perm_q, live_q = call(
-        functools.partial(first_local_kernel, peers), [SMEM, SMEM] + [ANY] * 15, [ANY] * 10, res,
+        functools.partial(first_local_kernel, peers), [SMEM, SMEM] + [ANY] * 13, [ANY] * 10, res,
         [vmem(x) for x in (src, dst, idx, vec, vec, nb)] + [pltpu.VMEM((slots, width), BF16), wts(5)]
         + [vmem(x) for x in (hf, nf, nf, hb, hb, onehot, onehot, onehot, live)] + [DMA(5), DMA(7), DMA(10)],
         2 * 10**9, 10**7,
-    )(sec, edge_count, src, dst, idx, node_feats, edge_feats, *own_w, *oth_w, vec, oth_vec)
-
-    args = (halo, pre_q, vec, oth_vec, live_q, oh_q, part, pre_n, e_q, lat, oh_s)
+    )(sec, edge_count, src, dst, idx, node_feats, edge_feats, *own_w[:3], *oth_w[:3], vec, oth_vec)
+
+    args = (halo, pre_q, vec, oth_vec, live_q, oh_q, part, e_q, pre_n, lat, oh_s)
     rows, n1, e1_q = call(
         functools.partial(first_finish_kernel, peers), [SMEM] + [ANY] * 19, [ANY] * 3, [msg, nb, hb],
         [vmem(x) for x in args] + [wts(4), tmp, vmem(msg), vmem(nb), vmem(hb), DMA(4), DMA(11), DMA(3)],
@@ -372,25 +394,25 @@
     halo = halo_exchange(rows)
 
     args = (n1, e1_q, e1_loc, oh_q, perm_q)
-    pre_q, part, pre_n, e1_h, out_l, n_out, e_out = call(
-        second_local_kernel, [SMEM, SMEM] + [ANY] * 17, [ANY] * 7, [hf, nf, nf, hb, hb] + outs,
+    pre_q, part, pre_n, e1_h, out_l, e_out = call(
+        second_local_kernel, [SMEM, SMEM] + [ANY] * 15, [ANY] * 6, [hf, nf, nf, hb, hb, outs[1]],
         [vmem(x) for x in (src, dst, vec, vec) + args] + [wts(5)] + [vmem(x) for x in (hf, nf, nf, hb, hb, hb)]
         + [DMA(5), DMA(9), DMA(6)],
         2 * 10**9, 10**7,
-    )(sec, edge_count, src, dst, *args, *own_w, *oth_w, vec, oth_vec)
+    )(sec, edge_count, src, dst, *args, *own_w[:3], *oth_w[:3], vec, oth_vec)
     oth_l = swap(out_l)
 
-    args = (halo, pre_q, vec, oth_vec, live_q, oh_q, part, pre_n, e1_q, n1, perm_q, e1_h, oth_l)
-    out_n, out_h, n_out, e_out = call(
-        functools.partial(last_finish_kernel, peers), [SMEM] + [ANY] * 23, [ANY] * 4, [nb, hb] + outs,
-        [vmem(x) for x in args] + [wts(4), tmp, vmem(nb), vmem(hb), DMA(4), DMA(13), DMA(5)],
-        10**9, 4 * 10**6, input_output_aliases={22: 2, 23: 3},
-    )(sec, *args, *own_w, *oth_w, n_out, e_out)
-    oth_h = swap(out_h)
-    oth_n = swap(out_n)
-
-    return call(other_out_kernel, [SMEM] + [VMEM] * 2 + [ANY, ANY], [ANY, ANY], outs, [DMA(2)], 0, 3 * 10**6,
-                limit=1024 * 1024, input_output_aliases={3: 0, 4: 1})(sec, oth_n, oth_h, n_out, e_out)
+    args = (halo, pre_q, vec, oth_vec, live_q, oh_q, part, e1_q, pre_n, n1, perm_q, e1_h, oth_l)
+    cross, n_out, e_out = call(
+        functools.partial(last_finish_kernel, peers), [SMEM] + [ANY] * 22, [ANY] * 3,
+        [shape((nodes + half, width), BF16)] + outs,
+        [vmem(x) for x in args] + [wts(4), tmp, vmem(hb), vmem(hb), vmem(nb), vmem(nb), DMA(4), DMA(13), DMA(5)],
+        10**9, 4 * 10**6, input_output_aliases={22: 2},
+    )(sec, *args, *own_w, *oth_w, e_out)
+    crossed = swap(cross)
+
+    return call(other_out_kernel, [SMEM, VMEM, ANY, ANY], [ANY, ANY], outs, [DMA(2)], 0, 3 * 10**6,
+                limit=1024 * 1024, input_output_aliases={2: 0, 3: 1})(sec, crossed, n_out, e_out)
 
 
 def solution(mesh):

time: 70.8 us -> 70.7 us (level)
    ppermute x8 -> x7, starting transfers between devices: 9.06 us -> 8.57 us  [swap(): return lax.ppermute(x, 'section', [(0, 1), (1, 0)])]
    ppermute x8 -> x7, waiting for transfers between devices: 3.54 us -> 3.64 us  [swap(): return lax.ppermute(x, 'section', [(0, 1), (1, 0)])]
  transfers between devices with their start and end apart: 10 -> 9, of which waited for: 6 -> 5; matrix products, arithmetic and copies ran while one was open for 0% -> 0% of each run, Pallas kernels for 19% -> 19%
where the time goes in v3:
time: 70.7 us; the launch traced here: 70.4 us
  starting transfers between devices  32.2 us (46%)
  Pallas kernels  24 us (34%)
  waiting for transfers between devices  12.1 us (17%)
  between operations  1.51 us (2%)
    all_to_all x2, starting transfers between devices, halo_exchange(): lax.all_to_all(m.reshape(peers, -1, 128), 'dom', split_axis=0, concat_axi...  23.7 us
    ppermute x7, starting transfers between devices, swap(): return lax.ppermute(x, 'section', [(0, 1), (1, 0)])  8.57 us
    all_to_all x2, waiting for transfers between devices, halo_exchange(): lax.all_to_all(m.reshape(peers, -1, 128), 'dom', split_axis=0, concat_axi...  8.45 us
    pallas_call x1, Pallas kernels, layers(): call(second_local_kernel, [SMEM, SMEM] + [ANY] * 15, [ANY] * 6, [hf, nf,...  6.04 us
    pallas_call x1, Pallas kernels, layers(): call(functools.partial(first_local_kernel, peers), [SMEM, SMEM] + [ANY] *...  5.4 us
    pallas_call x1, Pallas kernels, layers(): call(functools.partial(first_finish_kernel, peers), [SMEM] + [ANY] * 19,...  4.89 us
    pallas_call x1, Pallas kernels, layers(): call(functools.partial(last_finish_kernel, peers), [SMEM] + [ANY] * 22, [...  4.87 us
    ppermute x7, waiting for transfers between devices, swap(): return lax.ppermute(x, 'section', [(0, 1), (1, 0)])  3.64 us
  transfers between devices with their start and end apart: 9, of which 5 were waited for; matrix products, arithmetic and copies ran while one was open for 0% of the time, Pallas kernels for 19%

profile of v3, /device:TPU:1, one launch (start us, length us, event | category | flops | bytes accessed | tf_op | source)
XLA Modules:
  0.0 70.4 jit_solution(1279297595669525490)
XLA Ops:
  0.6 3.3 %collective-permute-start = (bf16[1,3,512,512]{3,2,1,0:T(8,128)(2,1)}, bf16[1,3,512,512]{3,2,1,0:T(8,128)(2,1)}, u32[]{:S(2)}, u32[]{:S(2)}) collective-permute-start(bf16[1,3,512,512]{3,2,1,0:T(8,128)(2,1)} %ew1.7), channel_id=1, source_target_pairs={{0,128},{128,0},{1,129},{129,1},{2,130},{130,2},{3,131},{131,3},{4... | collective-permute-start | bytes 4718600 | tf_op jit(solution)/shard_map/ppermute | solution.py:366
  3.9 0.1 collective-permute-start.2
  4.0 0.4 collective-permute-start.1
  4.4 0.1 collective-permute-start.4
  4.5 2.0 %shard_map.149 = (bf16[1024,128]{1,0:T(8,128)(2,1)}, bf16[4,512]{1,0:T(4,128)(2,1)}) custom-call(s32[1]{0:T(128)} %bitcast.sec, s32[2,128]{1,0:T(2,128)} %bitcast.10, bf16[2,256,512]{2,1,0:T(8,128)(2,1)} %nfeats.1, bf16[1,512]{1,0:T(2,128)(2,1)} %b0_h.1, bf16[1,512]{1,0:T(2,128)(2,1)} %b1_h.1, bf16[1,512]{1,0:T(2,128)(2,1)} %b2_h.1, bf16[1,512]{1,0:T(2,128)(2,1)} %b3_h.1), custom_call_target="tpu_custom_call" | custom-call | flops 100000000 | bytes 1000000 | tf_op jit(solution)/shard_map/pallas_call | solution.py:368
  6.6 14.3 %all-to-all-start = ((bf16[128,8,128]{2,1,0:T(8,128)(2,1)}), bf16[128,8,128]{2,1,0:T(8,128)(2,1)}, u32[]{:S(2)}, u32[]{:S(2)}) async-start(bf16[128,8,128]{2,1,0:T(8,128)(2,1)} %bitcast.8), calls=%async_computation | async-start | bytes 524288 | tf_op jit(solution)/shard_map/all_to_all | solution.py:362
  20.9 0.8 %collective-permute-start.3 = (bf16[4,512]{1,0:T(4,128)(2,1)}, bf16[4,512]{1,0:T(4,128)(2,1)S(1)}, u32[]{:S(2)}, u32[]{:S(2)}) collective-permute-start(bf16[4,512]{1,0:T(4,128)(2,1)} %get-tuple-element.27.vo_h), channel_id=1, source_target_pairs={{0,128},{128,0},{1,129},{129,1},{2,130},{130,2},{3,131},{131,3},{4... | collective-permute-start | bytes 12296 | tf_op jit(solution)/shard_map/ppermute | solution.py:366
  22.3 0.4 collective-permute-done.3.vx_h
  22.7 0.0 copy-start
  22.7 0.0 collective-permute-done.1.xew2
  22.7 0.0 collective-permute-done.2.xnw1
  22.7 0.0 collective-permute-done.xew1
  22.7 0.6 copy-done
  23.3 5.4 %shard_map.150 = (f32[256,512]{1,0:T(8,128)}, f32[256,512]{1,0:T(8,128)}, f32[256,512]{1,0:T(8,128)}, bf16[256,512]{1,0:T(8,128)(2,1)}, bf16[256,512]{1,0:T(8,12...) custom-call(s32[1]{0:T(128)} %bitcast.sec, ...), custom_call_target="tpu_custom_call" | custom-call | flops 2000000000 | bytes 10000000 | tf_op jit(solution)/shard_map/pallas_call | solution.py:381
  28.7 4.7 %all-to-all-done = bf16[128,8,128]{2,1,0:T(8,128)(2,1)} async-done(((bf16[128,8,128]{2,1,0:T(8,128)(2,1)}), bf16[128,8,128]{2,1,0:T(8,128)(2,1)}, u32[]{:S(2)}, u32[]{:S(2)}) %all-to-all-start) | async-done | bytes 262176 | tf_op jit(solution)/shard_map/all_to_all | solution.py:362
  33.4 0.0 collective-permute-done.4.xnw2
  33.4 4.9 %shard_map.151 = (bf16[1024,128]{1,0:T(8,128)(2,1)}, bf16[256,512]{1,0:T(8,128)(2,1)}, bf16[256,512]{1,0:T(8,128)(2,1)}) custom-call(s32[1]{0:T(128)} %bitcast.sec, bf16[1024,128]{1,0:T(8,128)(2,1)} %bitcast.3.msg_h, f32[256,512]{1,0:T(8,128)} %get-tuple-element.28.pre_q_h, bf16[4,512]{1,0:T(4,128)(2,1)} %get-tuple-element.27.vo_h, bf16[4,512]{1,0:T(4,128)(2,1)} %copy-done, ...), custom_call_target="tpu_custom_call" | custom-call | flops 1000000000 | bytes 4000000 | tf_op jit(solution)/shard_map/pallas_call | solution.py:389
  38.3 9.3 %all-to-all-start.1 = ((bf16[128,8,128]{2,1,0:T(8,128)(2,1)}), bf16[128,8,128]{2,1,0:T(8,128)(2,1)}, u32[]{:S(2)}, u32[]{:S(2)}) async-start(bf16[128,8,128]{2,1,0:T(8,128)(2,1)} %bitcast.9), calls=%async_computation.1 | async-start | bytes 524288 | tf_op jit(solution)/shard_map/all_to_all | solution.py:362
  47.7 6.0 %shard_map.152 = (f32[256,512]{1,0:T(8,128)}, f32[256,512]{1,0:T(8,128)}, f32[256,512]{1,0:T(8,128)}, bf16[256,512]{1,0:T(8,128)(2,1)}, bf16[256,512]{1,0:T(8,128)(2,1)}, /*index=5*/bf16[1,2,512,512]{3,2,1,0:T(8,128)(2,1)}) custom-call(s32[1]{0:T(128)} %bitcast.sec, s32[1]{0:T(128)S(6)} %copy.22.count, s32[1,512]{1,0:T(1,128)} %bitcast.13, ...), custom_call_target="tpu_custom_call" | custom-call | flops 2000000000 | bytes 10000000 | tf_op jit(solution)/shard_map/pallas_call | solution.py:397
  53.7 0.8 %collective-permute-start.5 = (bf16[256,512]{1,0:T(8,128)(2,1)}, bf16[256,512]{1,0:T(8,128)(2,1)}, u32[]{:S(2)}, u32[]{:S(2)}) collective-permute-start(bf16[256,512]{1,0:T(8,128)(2,1)} %get-tuple-element.45), channel_id=1, source_target_pairs={{0,128},{128,0},{1,129},{129,1},{2,130},{130,2},{3,131},{131,3},{4... | collective-permute-start | bytes 786440 | tf_op jit(solution)/shard_map/ppermute | solution.py:366
  54.5 1.5 %collective-permute-done.5.oth_l_h = bf16[256,512]{1,0:T(8,128)(2,1)} collective-permute-done((bf16[256,512]{1,0:T(8,128)(2,1)}, bf16[256,512]{1,0:T(8,128)(2,1)}, u32[]{:S(2)}, u32[]{:S(2)}) %collective-permute-start.5) | collective-permute-done | bytes 262176 | tf_op jit(solution)/shard_map/ppermute | solution.py:366
  56.0 3.7 %all-to-all-done.1 = bf16[128,8,128]{2,1,0:T(8,128)(2,1)} async-done(((bf16[128,8,128]{2,1,0:T(8,128)(2,1)}), bf16[128,8,128]{2,1,0:T(8,128)(2,1)}, u32[]{:S(2)}, u32[]{:S(2)}) %all-to-all-start.1) | async-done | bytes 262176 | tf_op jit(solution)/shard_map/all_to_all | solution.py:362
  59.8 4.9 %shard_map.153 = (bf16[512,512]{1,0:T(8,128)(2,1)}, bf16[1,2,256,512]{3,2,1,0:T(8,128)(2,1)}, bf16[1,2,512,512]{3,2,1,0:T(8,128)(2,1)}) custom-call(s32[1]{0:T(128)} %bitcast.sec, bf16[1024,128]{1,0:T(8,128)(2,1)} %bitcast.7.msg_h, f32[256,512]{1,0:T(8,128)} %get-tuple-element.41.pre_q_h, ...), custom_call_target="tpu_custom_call", output_to_operand_aliasing={{2}: (22, {})} | custom-call | flops 1000000000 | bytes 4000000 | tf_op jit(solution)/shard_map/pallas_call | solution.py:406
  64.6 3.1 %collective-permute-start.6 = (bf16[512,512]{1,0:T(8,128)(2,1)}, bf16[512,512]{1,0:T(8,128)(2,1)S(1)}, u32[]{:S(2)}, u32[]{:S(2)}) collective-permute-start(bf16[512,512]{1,0:T(8,128)(2,1)} %get-tuple-element.47), channel_id=1, source_target_pairs={{0,128},{128,0},{1,129},{129,1},{2,130},{130,2},{3,131},{131,3},{4... | collective-permute-start | bytes 1572872 | tf_op jit(solution)/shard_map/ppermute | solution.py:366
  67.7 1.7 %collective-permute-done.6.crossed = bf16[512,512]{1,0:T(8,128)(2,1)S(1)} collective-permute-done((bf16[512,512]{1,0:T(8,128)(2,1)}, bf16[512,512]{1,0:T(8,128)(2,1)S(1)}, u32[]{:S(2)}, u32[]{:S(2)}) %collective-permute-start.6) | collective-permute-done | bytes 524320 | tf_op jit(solution)/shard_map/ppermute | solution.py:366
  69.5 0.8 %shard_map.154 = (bf16[1,2,256,512]{3,2,1,0:T(8,128)(2,1)}, bf16[1,2,512,512]{3,2,1,0:T(8,128)(2,1)}) custom-call(s32[1]{0:T(128)} %bitcast.sec, bf16[512,512]{1,0:T(8,128)(2,1)S(1)} %collective-permute-done.6.crossed, bf16[1,2,256,512]{3,2,1,0:T(8,128)(2,1)} %get-tuple-element.48.n_in, ...), custom_call_target="tpu_custom_call", output_to_operand_aliasing={{0}: (2, {}), {1}: (3, {})} | custom-call | bytes 3000000 | tf_op jit(solution)/shard_map/pallas_call | solution.py:414
Async XLA Ops:
  0.6 22.1 %collective-permute-start = (bf16[1,3,512,512]{3,2,1,0:T(8,128)(2,1)}, bf16[1,3,512,512]{3,2,1,0:T(8,128)(2,1)}, u32[]{:S(2)}, u32[]{:S(2)}) collective-permute-start(bf16[1,3,512,512]{3,2,1,0:T(8,128)(2,1)} %ew1.7), channel_id=1, source_target_pairs={{0,128},{128,0},{1,129},{129,1},{2,130},{130,2},{3,131},{131,3},{4... | collective-permute-start | bytes 4718600 | tf_op jit(solution)/shard_map/ppermute | solution.py:366
  3.9 18.8 %collective-permute-start.2 = (bf16[1,2,512,512]{3,2,1,0:T(8,128)(2,1)}, bf16[1,2,512,512]{3,2,1,0:T(8,128)(2,1)}, u32[]{:S(2)}, u32[]{:S(2)}) collective-permute-start(bf16[1,2,512,512]{3,2,1,0:T(8,128)(2,1)} %nw1.7), channel_id=1, source_target_pairs={{0,128},{128,0},{1,129},{129,1},{2,130},{130,2},{3,131},{131,3},{4... | collective-permute-start | bytes 3145736 | tf_op jit(solution)/shard_map/ppermute | solution.py:366
  4.0 18.7 %collective-permute-start.1 = (bf16[1,512,512]{2,1,0:T(8,128)(2,1)}, bf16[1,512,512]{2,1,0:T(8,128)(2,1)}, u32[]{:S(2)}, u32[]{:S(2)}) collective-permute-start(bf16[1,512,512]{2,1,0:T(8,128)(2,1)} %ew2.7), channel_id=1, source_target_pairs={{0,128},{128,0},{1,129},{129,1},{2,130},{130,2},{3,131},{131,3},{4... | collective-permute-start | bytes 1572872 | tf_op jit(solution)/shard_map/ppermute | solution.py:366
  4.4 29.0 %collective-permute-start.4 = (bf16[1,512,512]{2,1,0:T(8,128)(2,1)}, bf16[1,512,512]{2,1,0:T(8,128)(2,1)}, u32[]{:S(2)}, u32[]{:S(2)}) collective-permute-start(bf16[1,512,512]{2,1,0:T(8,128)(2,1)} %nw2.3), channel_id=1, source_target_pairs={{0,128},{128,0},{1,129},{129,1},{2,130},{130,2},{3,131},{131,3},{4... | collective-permute-start | bytes 1572872 | tf_op jit(solution)/shard_map/ppermute | solution.py:366
  6.6 26.9 %all-to-all-start = ((bf16[128,8,128]{2,1,0:T(8,128)(2,1)}), bf16[128,8,128]{2,1,0:T(8,128)(2,1)}, u32[]{:S(2)}, u32[]{:S(2)}) async-start(bf16[128,8,128]{2,1,0:T(8,128)(2,1)} %bitcast.8), calls=%async_computation | async-start | bytes 524288 | tf_op jit(solution)/shard_map/all_to_all | solution.py:362
  20.9 1.8 %collective-permute-start.3 = (bf16[4,512]{1,0:T(4,128)(2,1)}, bf16[4,512]{1,0:T(4,128)(2,1)S(1)}, u32[]{:S(2)}, u32[]{:S(2)}) collective-permute-start(bf16[4,512]{1,0:T(4,128)(2,1)} %get-tuple-element.27.vo_h), channel_id=1, source_target_pairs={{0,128},{128,0},{1,129},{129,1},{2,130},{130,2},{3,131},{131,3},{4... | collective-permute-start | bytes 12296 | tf_op jit(solution)/shard_map/ppermute | solution.py:366
  22.7 0.6 copy-start
  38.3 21.4 %all-to-all-start.1 = ((bf16[128,8,128]{2,1,0:T(8,128)(2,1)}), bf16[128,8,128]{2,1,0:T(8,128)(2,1)}, u32[]{:S(2)}, u32[]{:S(2)}) async-start(bf16[128,8,128]{2,1,0:T(8,128)(2,1)} %bitcast.9), calls=%async_computation.1 | async-start | bytes 524288 | tf_op jit(solution)/shard_map/all_to_all | solution.py:362
  53.7 2.3 %collective-permute-start.5 = (bf16[256,512]{1,0:T(8,128)(2,1)}, bf16[256,512]{1,0:T(8,128)(2,1)}, u32[]{:S(2)}, u32[]{:S(2)}) collective-permute-start(bf16[256,512]{1,0:T(8,128)(2,1)} %get-tuple-element.45), channel_id=1, source_target_pairs={{0,128},{128,0},{1,129},{129,1},{2,130},{130,2},{3,131},{131,3},{4... | collective-permute-start | bytes 786440 | tf_op jit(solution)/shard_map/ppermute | solution.py:366
  64.6 4.8 %collective-permute-start.6 = (bf16[512,512]{1,0:T(8,128)(2,1)}, bf16[512,512]{1,0:T(8,128)(2,1)S(1)}, u32[]{:S(2)}, u32[]{:S(2)}) collective-permute-start(bf16[512,512]{1,0:T(8,128)(2,1)} %get-tuple-element.47), channel_id=1, source_target_pairs={{0,128},{128,0},{1,129},{129,1},{2,130},{130,2},{3,131},{131,3},{4... | collective-permute-start | bytes 1572872 | tf_op jit(solution)/shard_map/ppermute | solution.py:366
